TPU v7x, 32 devices: a whole 2x2x4 slice. The times are simulated.
32 devices in a mesh: dp: 8 (over z, x), seq: 4 (over y, core).
Axes of the slice: x: 2, y: 2, z: 4, core: 2. Of those that a mesh axis runs over, the one named last changes fastest.
Arguments:
- tokens: bfloat16 [12288, 1024], P(('dp', 'seq')), may hold values from -6 to 6
- lengths: int32 [8], P('dp'), may hold values from 193 to 1536, as said below
- cotangent: bfloat16 [12288, 1024], P(('dp', 'seq')), may hold values from -12 to 12
- ln1_gain: bfloat16 [1024], P(('dp', 'seq')), may hold values from 0.25 to 1.75
- ln1_shift: bfloat16 [1024], P(('dp', 'seq')), may hold values from -1.75 to 1.75
- w_qkv: bfloat16 [1024, 3, 1024], P('dp', None, 'seq'), may hold values from -0.1875 to 0.1875
- b_qv: bfloat16 [2048], P(('dp', 'seq')), may hold values from -1.75 to 1.75
- w_out: bfloat16 [1024, 1024], P('seq', 'dp'), may hold values from -0.5 to 0.5
- b_out: bfloat16 [1024], P(('dp', 'seq')), may hold values from -1.75 to 1.75
- ln2_gain: bfloat16 [1024], P(('dp', 'seq')), may hold values from 0.25 to 1.75
- ln2_shift: bfloat16 [1024], P(('dp', 'seq')), may hold values from -1.75 to 1.75
- w_fc1: bfloat16 [1024, 4096], P('dp', 'seq'), may hold values from -0.1875 to 0.1875
- b_fc1: bfloat16 [4096], P(('dp', 'seq')), may hold values from -3 to 3
- w_fc2: bfloat16 [4096, 1024], P('seq', 'dp'), may hold values from -0.125 to 0.125
- b_fc2: bfloat16 [1024], P(('dp', 'seq')), may hold values from -1.75 to 1.75
Outputs:
- output: bfloat16 [12288, 1024], P(('dp', 'seq'))
- grad_tokens: bfloat16 [12288, 1024], P(('dp', 'seq'))
- grad_ln1_gain: float32 [1024], P(('dp', 'seq'))
- grad_ln1_shift: float32 [1024], P(('dp', 'seq'))
- grad_w_qkv: float32 [1024, 3, 1024], P('dp', None, 'seq')
- grad_b_qv: float32 [2048], P(('dp', 'seq'))
- grad_w_out: float32 [1024, 1024], P('seq', 'dp')
- grad_b_out: float32 [1024], P(('dp', 'seq'))
- grad_ln2_gain: float32 [1024], P(('dp', 'seq'))
- grad_ln2_shift: float32 [1024], P(('dp', 'seq'))
- grad_w_fc1: float32 [1024, 4096], P('dp', 'seq')
- grad_b_fc1: float32 [4096], P(('dp', 'seq'))
- grad_w_fc2: float32 [4096, 1024], P('seq', 'dp')
- grad_b_fc2: float32 [1024], P(('dp', 'seq'))
Inputs may be any that keep to these rules, and one draw needn't show every extreme that they name: `lengths`: some sequence has length 1536 and some has length 193.
All inputs are finite; a program needn't handle non-finite values.
Results may differ from a plain program's by a relative error of at most 0.014.
Values may be sent and summed in bfloat16 or wider, within the bound.
A program may use at most 192 MiB of HBM per device.

v0:
```python
import functools
import math

import jax
import jax.numpy as jnp
from jax import lax
from jax.experimental import pallas as pl
from jax.experimental.pallas import tpu as pltpu
from jax.sharding import PartitionSpec as P

HEAD_DIM = 64
EPS = 1e-05
GELU_COEF = 0.044715
NEG = -1e30
LANES = 128
VMEM_BYTES = 60 * 1024 * 1024

f32 = jnp.float32
bf16 = jnp.bfloat16
WHOLE = pl.BlockSpec(memory_space=pltpu.VMEM)
SCALAR = pl.BlockSpec(memory_space=pltpu.SMEM)


def mm(a, b):
    return jnp.dot(a, b, preferred_element_type=f32)


def mm_t(a, b):
    return lax.dot_general(a, b, (((1,), (1,)), ((), ())), preferred_element_type=f32)


def params(**kw):
    return pltpu.CompilerParams(vmem_limit_bytes=VMEM_BYTES, **kw)


def normalize(v):
    width = v.shape[-1]
    centred = v - jnp.sum(v, axis=-1, keepdims=True) * (1.0 / width)
    inv = lax.rsqrt(jnp.sum(centred * centred, axis=-1, keepdims=True) * (1.0 / width) + EPS)
    return centred * inv, inv


def norm_back(grad_out, gain, unit, inv):
    width = unit.shape[-1]
    scaled = grad_out * gain
    mean_one = jnp.sum(scaled, axis=-1, keepdims=True) * (1.0 / width)
    mean_two = jnp.sum(scaled * unit, axis=-1, keepdims=True) * (1.0 / width)
    return inv * (scaled - mean_one - unit * mean_two)


def device_of(index, seq_n):
    return (index // seq_n, index % seq_n)


def greet_all(me, count, seq_n):
    barrier = pltpu.get_barrier_semaphore()

    def hello(i, carry):
        peer = (me + i) % count
        pl.semaphore_signal(
            barrier, inc=1, device_id=device_of(peer, seq_n), device_id_type=pl.DeviceIdType.MESH
        )
        return carry

    lax.fori_loop(1, count, hello, 0)
    pl.semaphore_wait(barrier, count - 1)


def small_gather_body(count, seq_n, x_ref, out_ref, send_sem, recv_sem):
    me = lax.axis_index("dp") * seq_n + lax.axis_index("seq")
    greet_all(me, count, seq_n)

    def copy_to(i):
        peer = (me + i) % count
        return pltpu.make_async_remote_copy(
            src_ref=x_ref,
            dst_ref=out_ref.at[pl.ds(me, 1)],
            send_sem=send_sem.at[i],
            recv_sem=recv_sem.at[i],
            device_id=device_of(peer, seq_n),
            device_id_type=pl.DeviceIdType.MESH,
        )

    def begin(i, carry):
        copy_to(i).start()
        return carry

    def finish(i, carry):
        copy_to(i).wait()
        return carry

    lax.fori_loop(1, count, begin, 0)
    out_ref[pl.ds(me, 1)] = x_ref[...]
    lax.fori_loop(1, count, finish, 0)


def small_gather(x, count, seq_n):
    width = x.shape[-1]
    return pl.pallas_call(
        functools.partial(small_gather_body, count, seq_n),
        out_shape=jax.ShapeDtypeStruct((count, 1, width), f32),
        in_specs=[WHOLE],
        out_specs=WHOLE,
        scratch_shapes=[pltpu.SemaphoreType.DMA((count,)), pltpu.SemaphoreType.DMA((count,))],
        compiler_params=pltpu.CompilerParams(collective_id=1, has_side_effects=True),
        name="small_gather",
    )(x.reshape(1, 1, width))


def small_scatter_body(count, seq_n, v_ref, out_ref, land, send_sem, recv_sem):
    me = lax.axis_index("dp") * seq_n + lax.axis_index("seq")
    greet_all(me, count, seq_n)

    def copy_to(i):
        peer = (me + i) % count
        return pltpu.make_async_remote_copy(
            src_ref=v_ref.at[pl.ds(peer, 1)],
            dst_ref=land.at[pl.ds(i, 1)],
            send_sem=send_sem.at[i],
            recv_sem=recv_sem.at[i],
            device_id=device_of(peer, seq_n),
            device_id_type=pl.DeviceIdType.MESH,
        )

    def begin(i, carry):
        copy_to(i).start()
        return carry

    def finish(i, total):
        copy_to(i).wait()
        return total + land[pl.ds(i, 1)]

    lax.fori_loop(1, count, begin, 0)
    out_ref[...] = lax.fori_loop(1, count, finish, v_ref[pl.ds(me, 1)])


def small_scatter(v, count, seq_n):
    width = v.shape[-1]
    return pl.pallas_call(
        functools.partial(small_scatter_body, count, seq_n),
        out_shape=jax.ShapeDtypeStruct((1, 1, width), f32),
        in_specs=[WHOLE],
        out_specs=WHOLE,
        scratch_shapes=[
            pltpu.VMEM((count, 1, width), f32),
            pltpu.SemaphoreType.DMA((count,)),
            pltpu.SemaphoreType.DMA((count,)),
        ],
        compiler_params=pltpu.CompilerParams(collective_id=2, has_side_effects=True),
        name="small_scatter",
    )(v.reshape(count, 1, width))


def swap(x, bit):
    return lax.ppermute(x, "seq", [(i, i ^ bit) for i in range(4)])


def spread(own):
    far = swap(own, 2)
    return own, swap(own, 1), far, swap(far, 1)


def reduce_rows(near, far):
    got = swap(near, 1)
    across = swap(far[0] + got[1], 2)
    return got, across


def pick(step, refs, dest):
    for k, ref in enumerate(refs):

        @pl.when(step == k)
        def _(ref=ref):
            dest[...] = ref[...]


ORDER = (1, 3, 2, 0)


def rel_of(t):
    return jnp.where(t == 0, 1, jnp.where(t == 1, 3, jnp.where(t == 2, 2, 0)))


def qkv_body(scal, x0, x1, x2, x3, w, gain, shift, bias, h1, qkv, rows):
    pick(pl.program_id(0), (x0, x1, x2, x3), rows)
    unit, _ = normalize(rows[...].astype(f32))
    low = (unit * gain[...] + shift[...]).astype(bf16)
    h1[...] = low
    qkv[...] = (mm(low, w[...]) + bias[...]).astype(bf16)


def qkv_call(scal, pieces, w, gain, shift, bias):
    rows, width = pieces[0].shape
    cols = w.shape[1]
    out = lambda r, sc: (lax.bitwise_xor(sc[0], r), 0)
    return pl.pallas_call(
        qkv_body,
        out_shape=(
            jax.ShapeDtypeStruct((4 * rows, width), bf16),
            jax.ShapeDtypeStruct((4 * rows, cols), bf16),
        ),
        grid_spec=pltpu.PrefetchScalarGridSpec(
            num_scalar_prefetch=1,
            grid=(4,),
            in_specs=[WHOLE] * 8,
            out_specs=(pl.BlockSpec((rows, width), out), pl.BlockSpec((rows, cols), out)),
            scratch_shapes=[pltpu.VMEM((rows, width), bf16)],
        ),
        compiler_params=params(),
        name="qkv",
    )(scal, *pieces, w, gain, shift, bias)


def make_bias(scal, slopes, pair, bias, keys):
    pos = lax.broadcasted_iota(jnp.int32, (keys, LANES), 0)
    inside = pos < scal[1]
    ramp = pos.astype(f32)
    for h in range(2):
        bias[h] = jnp.where(inside, ramp * slopes[2 * pair + h], NEG)


def head_only(x, h):
    lane = lax.broadcasted_iota(jnp.int32, x.shape, 1)
    return jnp.where((lane >= h * HEAD_DIM) & (lane < (h + 1) * HEAD_DIM), x, jnp.zeros_like(x))


def score_t(k_ref, qm, bias, h, length):
    block = qm.shape[0]
    s = mm_t(k_ref[0:length, :], qm)
    b = bias[h, 0:length, :]
    s = s + jnp.concatenate([b] * (block // LANES), axis=1)
    key = lax.broadcasted_iota(jnp.int32, (block, block), 0)
    query = lax.broadcasted_iota(jnp.int32, (block, block), 1)
    last = jnp.where(key <= query, s[length - block :], NEG)
    if length == block:
        return last
    return jnp.concatenate([s[: length - block], last], axis=0)


def attend_body(scal, q, k, v, slopes, o, lse, bias, vt):
    pair, step = pl.program_id(0), pl.program_id(1)
    block = q.shape[0]
    keys = k.shape[0]

    @pl.when(step == 0)
    def _():
        make_bias(scal, slopes, pair, bias, keys)
        vt[...] = v[...].T

    for c in range(keys // block):

        @pl.when(step == c)
        def _(c=c):
            length = (c + 1) * block
            scaled = q[...] * bf16(HEAD_DIM**-0.5)
            outs, logs = [], []
            for h in range(2):
                s = score_t(k, head_only(scaled, h), bias, h, length)
                top = jnp.max(s, axis=0, keepdims=True)
                e = jnp.exp(s - top)
                total = jnp.sum(e, axis=0, keepdims=True)
                mixed = mm(vt[h * HEAD_DIM : (h + 1) * HEAD_DIM, 0:length], e.astype(bf16))
                outs.append(mixed / total)
                logs.append(top + jnp.log(total))
            o[...] = jnp.concatenate(outs, axis=0).T.astype(bf16)
            lse[0, 0:2, :] = jnp.concatenate(logs, axis=0)


def attend_call(scal, slopes, qkv, block):
    keys, cols = qkv.shape
    width = cols // 3
    pairs = width // LANES
    return pl.pallas_call(
        attend_body,
        out_shape=(
            jax.ShapeDtypeStruct((keys, width), bf16),
            jax.ShapeDtypeStruct((pairs, 8, keys), f32),
        ),
        grid_spec=pltpu.PrefetchScalarGridSpec(
            num_scalar_prefetch=1,
            grid=(pairs, keys // block),
            in_specs=[
                pl.BlockSpec((block, LANES), lambda p, c, sc: (c, p)),
                pl.BlockSpec((keys, LANES), lambda p, c, sc: (0, pairs + p)),
                pl.BlockSpec((keys, LANES), lambda p, c, sc: (0, 2 * pairs + p)),
                SCALAR,
            ],
            out_specs=(
                pl.BlockSpec((block, LANES), lambda p, c, sc: (c, p)),
                pl.BlockSpec((1, 8, block), lambda p, c, sc: (p, 0, c)),
            ),
            scratch_shapes=[
                pltpu.VMEM((2, keys, LANES), f32),
                pltpu.VMEM((LANES, keys), bf16),
            ],
        ),
        compiler_params=params(),
        name="attend",
    )(scal, qkv, qkv, qkv, slopes)


def attend_back_body(scal, q, k, v, o, do, lse, slopes, dq, dk, dv, bias, kt, dk_sum, dv_sum):
    pair, step = pl.program_id(0), pl.program_id(1)
    block = q.shape[0]
    keys = k.shape[0]
    scale = HEAD_DIM**-0.5

    @pl.when(step == 0)
    def _():
        make_bias(scal, slopes, pair, bias, keys)
        kt[...] = k[...].T
        dk_sum[...] = jnp.zeros_like(dk_sum)
        dv_sum[...] = jnp.zeros_like(dv_sum)

    for c in range(keys // block):

        @pl.when(step == c)
        def _(c=c):
            length = (c + 1) * block
            scaled = q[...] * bf16(scale)
            both = (do[...].astype(f32) * o[...].astype(f32)).T
            outs = []
            for h in range(2):
                qm = head_only(scaled, h)
                dom = head_only(do[...], h)
                dot_row = jnp.sum(both[h * HEAD_DIM : (h + 1) * HEAD_DIM], axis=0, keepdims=True)
                p = jnp.exp(score_t(k, qm, bias, h, length) - lse[0, h : h + 1, :])
                dp = mm_t(v[0:length, :], dom)
                ds = (p * (dp - dot_row)).astype(bf16)
                dv_sum[0:length, :] += mm(p.astype(bf16), dom)
                dk_sum[0:length, :] += mm(ds, qm)
                outs.append(mm(kt[h * HEAD_DIM : (h + 1) * HEAD_DIM, 0:length], ds))
            dq[...] = (jnp.concatenate(outs, axis=0).T * scale).astype(bf16)

    @pl.when(step == keys // block - 1)
    def _():
        dk[...] = dk_sum[...].astype(bf16)
        dv[...] = dv_sum[...].astype(bf16)


def attend_back_call(scal, slopes, qkv, o, do, lse, block):
    keys, cols = qkv.shape
    width = cols // 3
    pairs = width // LANES
    some = pl.BlockSpec((block, LANES), lambda p, c, sc: (c, p))
    full = pl.BlockSpec((keys, LANES), lambda p, c, sc: (0, p))
    return pl.pallas_call(
        attend_back_body,
        out_shape=(jax.ShapeDtypeStruct((keys, width), bf16),) * 3,
        grid_spec=pltpu.PrefetchScalarGridSpec(
            num_scalar_prefetch=1,
            grid=(pairs, keys // block),
            in_specs=[
                some,
                pl.BlockSpec((keys, LANES), lambda p, c, sc: (0, pairs + p)),
                pl.BlockSpec((keys, LANES), lambda p, c, sc: (0, 2 * pairs + p)),
                some,
                some,
                pl.BlockSpec((1, 8, block), lambda p, c, sc: (p, 0, c)),
                SCALAR,
            ],
            out_specs=(some, full, full),
            scratch_shapes=[
                pltpu.VMEM((2, keys, LANES), f32),
                pltpu.VMEM((LANES, keys), bf16),
                pltpu.VMEM((keys, LANES), f32),
                pltpu.VMEM((keys, LANES), f32),
            ],
        ),
        compiler_params=params(),
        name="attend_back",
    )(scal, qkv, qkv, qkv, o, do, lse, slopes)


def lay_columns(w_ref, first, dest):
    width = w_ref.shape[2]
    for d in range(w_ref.shape[0]):
        dest[:, d * width : (d + 1) * width] = w_ref[d, first : first + dest.shape[0], :]


def out_body(scal, o, w, near, far, flat, *, first):
    t = pl.program_id(0)

    @pl.when(t == 0)
    def _():
        lay_columns(w, first, flat)

    part = mm(o[...], flat[...]).astype(bf16)

    @pl.when(t < 2)
    def _():
        near[0] = part

    @pl.when(t >= 2)
    def _():
        far[0] = part


def near_map(t, *_):
    return (jnp.minimum(t, 1), 0, 0)


def far_map(t, *_):
    return (jnp.maximum(t - 2, 0), 0, 0)


def out_call(scal, o, w, first):
    keys, inner = o.shape
    rows = keys // 4
    width = w.shape[0] * w.shape[2]
    return pl.pallas_call(
        functools.partial(out_body, first=first),
        out_shape=(jax.ShapeDtypeStruct((2, rows, width), bf16),) * 2,
        grid_spec=pltpu.PrefetchScalarGridSpec(
            num_scalar_prefetch=1,
            grid=(4,),
            in_specs=[
                pl.BlockSpec((rows, inner), lambda t, sc: (lax.bitwise_xor(sc[0], rel_of(t)), 0)),
                WHOLE,
            ],
            out_specs=(
                pl.BlockSpec((1, rows, width), near_map),
                pl.BlockSpec((1, rows, width), far_map),
            ),
            scratch_shapes=[pltpu.VMEM((inner, width), bf16)],
        ),
        compiler_params=params(),
        name="out_proj",
    )(scal, o, w)


def mid_body(x, a, b, c, bias, gain, shift, mid, h2):
    value = x[...].astype(f32) + (
        (a[0].astype(f32) + b[0].astype(f32)) + c[...].astype(f32) + bias[...]
    )
    mid[...] = value
    unit, _ = normalize(value)
    h2[...] = (unit * gain[...] + shift[...]).astype(bf16)


def mid_call(x, a, b, c, bias, gain, shift):
    rows, width = x.shape
    one = pl.BlockSpec((rows // 2, width), lambda i: (i, 0))
    first = pl.BlockSpec((1, rows // 2, width), lambda i: (0, i, 0))
    second = pl.BlockSpec((1, rows // 2, width), lambda i: (1, i, 0))
    row = pl.BlockSpec((1, width), lambda i: (0, 0))
    return pl.pallas_call(
        mid_body,
        out_shape=(
            jax.ShapeDtypeStruct((rows, width), f32),
            jax.ShapeDtypeStruct((rows, width), bf16),
        ),
        grid=(2,),
        in_specs=[one, second, first, one, row, row, row],
        out_specs=(one, one),
        compiler_params=params(),
        name="mid_norm",
    )(x, a, b, c, bias, gain, shift)


def gelu_parts(u):
    root = math.sqrt(2.0 / math.pi)
    sq = u * u
    t = jnp.tanh(root * (u + GELU_COEF * (sq * u)))
    half = 0.5 * (1.0 + t)
    slope = half + 0.5 * u * (1.0 - t * t) * (root * (1.0 + 3.0 * GELU_COEF * sq))
    return u * half, slope


def mlp_body(
    h0, h1, h2, h3, g_rows, w1, w2, b1,
    y_near, y_far, d_near, d_far, a_all, du_all, h_all, g_all, bias_sum,
    flat, hb, gb,
):
    t = pl.program_id(0)

    @pl.when(t == 0)
    def _():
        lay_columns(w2, 0, flat)
        bias_sum[...] = jnp.zeros_like(bias_sum)

    pick(rel_of(t), (h0, h1, h2, h3), hb)
    gb[...] = g_rows[rel_of(t)]
    h_all[...] = hb[...]
    g_all[...] = gb[...]
    inner = w1.shape[1]
    chunk = 256
    for c in range(inner // chunk):
        cols = slice(c * chunk, (c + 1) * chunk)
        u = mm(hb[...], w1[:, cols]) + b1[:, cols]
        value, slope = gelu_parts(u)
        a_all[:, cols] = value.astype(bf16)
        du = (mm_t(gb[...], flat[cols, :]) * slope).astype(bf16)
        du_all[:, cols] = du
        bias_sum[:, cols] += jnp.sum(du.astype(f32), axis=0, keepdims=True)
    y = mm(a_all[...], flat[...]).astype(bf16)
    d = mm_t(du_all[...], w1[...]).astype(bf16)

    @pl.when(t < 2)
    def _():
        y_near[0] = y
        d_near[0] = d

    @pl.when(t >= 2)
    def _():
        y_far[0] = y
        d_far[0] = d


def mlp_call(h_pieces, g_rows, w1, w2, b1):
    rows, width = h_pieces[0].shape
    inner = w1.shape[1]
    pair = jax.ShapeDtypeStruct((2, rows, width), bf16)
    near = pl.BlockSpec((1, rows, width), near_map)
    far = pl.BlockSpec((1, rows, width), far_map)
    block = lambda n: pl.BlockSpec((rows, n), lambda t: (t, 0))
    return pl.pallas_call(
        mlp_body,
        out_shape=(
            pair,
            pair,
            pair,
            pair,
            jax.ShapeDtypeStruct((4 * rows, inner), bf16),
            jax.ShapeDtypeStruct((4 * rows, inner), bf16),
            jax.ShapeDtypeStruct((4 * rows, width), bf16),
            jax.ShapeDtypeStruct((4 * rows, width), bf16),
            jax.ShapeDtypeStruct((1, inner), f32),
        ),
        grid=(4,),
        in_specs=[WHOLE] * 8,
        out_specs=(
            near, far, near, far, block(inner), block(inner), block(width), block(width),
            pl.BlockSpec((1, inner), lambda t: (0, 0)),
        ),
        scratch_shapes=[
            pltpu.VMEM((inner, width), bf16),
            pltpu.VMEM((rows, width), bf16),
            pltpu.VMEM((rows, width), bf16),
        ],
        compiler_params=params(),
        name="mlp",
    )(*h_pieces, g_rows, w1, w2, b1)


def outer_body(left, right, out, turned, *, blocks):
    @pl.when(pl.program_id(0) == 0)
    def _():
        turned[...] = left[...].T

    part = mm(turned[...], right[...]).astype(bf16)
    if blocks:
        width = out.shape[2]
        for d in range(out.shape[0]):
            out[d] = part[:, d * width : (d + 1) * width]
    else:
        out[...] = part


def outer_call(left, right, parts, name):
    rows, m = left.shape
    n = right.shape[1]
    step = 256
    if parts > 1:
        width = n // parts
        out_shape = jax.ShapeDtypeStruct((parts, m, width), bf16)
        out_spec = pl.BlockSpec((step // width, m, width), lambda j: (j, 0, 0))
    else:
        out_shape = jax.ShapeDtypeStruct((m, n), bf16)
        out_spec = pl.BlockSpec((m, step), lambda j: (0, j))
    return pl.pallas_call(
        functools.partial(outer_body, blocks=parts > 1),
        out_shape=out_shape,
        grid=(n // step,),
        in_specs=[WHOLE, pl.BlockSpec((rows, step), lambda j: (0, j))],
        out_specs=out_spec,
        scratch_shapes=[pltpu.VMEM((m, rows), bf16)],
        compiler_params=params(),
        name=name,
    )(left, right)


def mid_back_body(mid, a, b, c, g, gain, dmid, dbr, sums):
    @pl.when(pl.program_id(0) == 0)
    def _():
        sums[...] = jnp.zeros_like(sums)

    unit, inv = normalize(mid[...])
    e = (a[0].astype(f32) + b[0].astype(f32)) + c[...].astype(f32)
    grad = g[...].astype(f32)
    value = grad + norm_back(e, gain[...], unit, inv)
    dmid[...] = value
    low = value.astype(bf16)
    dbr[...] = low
    sums[0:1, :] += jnp.sum(e * unit, axis=0, keepdims=True)
    sums[1:2, :] += jnp.sum(e, axis=0, keepdims=True)
    sums[2:3, :] += jnp.sum(low.astype(f32), axis=0, keepdims=True)
    sums[3:4, :] += jnp.sum(grad, axis=0, keepdims=True)


def mid_back_call(mid, a, b, c, g, gain):
    rows, width = mid.shape
    one = pl.BlockSpec((rows // 2, width), lambda i: (i, 0))
    first = pl.BlockSpec((1, rows // 2, width), lambda i: (0, i, 0))
    second = pl.BlockSpec((1, rows // 2, width), lambda i: (1, i, 0))
    row = pl.BlockSpec((1, width), lambda i: (0, 0))
    return pl.pallas_call(
        mid_back_body,
        out_shape=(
            jax.ShapeDtypeStruct((rows, width), f32),
            jax.ShapeDtypeStruct((rows, width), bf16),
            jax.ShapeDtypeStruct((8, width), f32),
        ),
        grid=(2,),
        in_specs=[one, second, first, one, one, row],
        out_specs=(one, one, pl.BlockSpec((8, width), lambda i: (0, 0))),
        compiler_params=params(),
        name="mid_back",
    )(mid, a, b, c, g, gain)


def out_back_body(scal, b0, b1, b2, b3, o, w, do, grad, flat, rows, total, *, first):
    r = pl.program_id(0)

    @pl.when(r == 0)
    def _():
        lay_columns(w, first, flat)
        total[...] = jnp.zeros_like(total)

    pick(r, (b0, b1, b2, b3), rows)
    do[...] = mm_t(rows[...], flat[...]).astype(bf16)
    total[...] += mm(o[...].T, rows[...])

    @pl.when(r == 3)
    def _():
        width = grad.shape[2]
        for d in range(grad.shape[0]):
            grad[d] = total[:, d * width : (d + 1) * width].astype(bf16)


def out_back_call(scal, pieces, o, w, first):
    rows, width = pieces[0].shape
    inner = o.shape[1]
    at = pl.BlockSpec((rows, inner), lambda r, sc: (lax.bitwise_xor(sc[0], r), 0))
    grad = (w.shape[0], inner, w.shape[2])
    return pl.pallas_call(
        functools.partial(out_back_body, first=first),
        out_shape=(jax.ShapeDtypeStruct(o.shape, bf16), jax.ShapeDtypeStruct(grad, bf16)),
        grid_spec=pltpu.PrefetchScalarGridSpec(
            num_scalar_prefetch=1,
            grid=(4,),
            in_specs=[WHOLE] * 4 + [at, WHOLE],
            out_specs=(at, pl.BlockSpec(grad, lambda r, sc: (0, 0, 0))),
            scratch_shapes=[
                pltpu.VMEM((inner, width), bf16),
                pltpu.VMEM((rows, width), bf16),
                pltpu.VMEM((inner, width), f32),
            ],
        ),
        compiler_params=params(),
        name="out_back",
    )(scal, *pieces, o, w)


def qkv_back_body(scal, dq, dk, dv, w, near, far, merged, sums):
    t = pl.program_id(0)

    @pl.when(t == 0)
    def _():
        sums[...] = jnp.zeros_like(sums)

    low = jnp.concatenate([dq[...], dk[...], dv[...]], axis=1)
    merged[...] = low
    part = mm_t(low, w[...]).astype(bf16)
    sums[...] += jnp.sum(low.astype(f32), axis=0, keepdims=True)

    @pl.when(t < 2)
    def _():
        near[0] = part

    @pl.when(t >= 2)
    def _():
        far[0] = part


def qkv_back_call(scal, dq, dk, dv, w):
    keys, inner = dq.shape
    rows = keys // 4
    width = w.shape[0]
    where = lambda t, sc: (lax.bitwise_xor(sc[0], rel_of(t)), 0)
    at = pl.BlockSpec((rows, inner), where)
    return pl.pallas_call(
        qkv_back_body,
        out_shape=(
            jax.ShapeDtypeStruct((2, rows, width), bf16),
            jax.ShapeDtypeStruct((2, rows, width), bf16),
            jax.ShapeDtypeStruct((keys, 3 * inner), bf16),
            jax.ShapeDtypeStruct((1, 3 * inner), f32),
        ),
        grid_spec=pltpu.PrefetchScalarGridSpec(
            num_scalar_prefetch=1,
            grid=(4,),
            in_specs=[at, at, at, WHOLE],
            out_specs=(
                pl.BlockSpec((1, rows, width), near_map),
                pl.BlockSpec((1, rows, width), far_map),
                pl.BlockSpec((rows, 3 * inner), where),
                pl.BlockSpec((1, 3 * inner), lambda t, sc: (0, 0)),
            ),
        ),
        compiler_params=params(),
        name="qkv_back",
    )(scal, dq, dk, dv, w)


def in_back_body(x, a, b, c, dmid, gain, grad, sums):
    @pl.when(pl.program_id(0) == 0)
    def _():
        sums[...] = jnp.zeros_like(sums)

    unit, inv = normalize(x[...].astype(f32))
    e = (a[0].astype(f32) + b[0].astype(f32)) + c[...].astype(f32)
    grad[...] = (dmid[...] + norm_back(e, gain[...], unit, inv)).astype(bf16)
    sums[0:1, :] += jnp.sum(e * unit, axis=0, keepdims=True)
    sums[1:2, :] += jnp.sum(e, axis=0, keepdims=True)


def in_back_call(x, a, b, c, dmid, gain):
    rows, width = x.shape
    one = pl.BlockSpec((rows // 2, width), lambda i: (i, 0))
    first = pl.BlockSpec((1, rows // 2, width), lambda i: (0, i, 0))
    second = pl.BlockSpec((1, rows // 2, width), lambda i: (1, i, 0))
    row = pl.BlockSpec((1, width), lambda i: (0, 0))
    return pl.pallas_call(
        in_back_body,
        out_shape=(
            jax.ShapeDtypeStruct((rows, width), bf16),
            jax.ShapeDtypeStruct((8, width), f32),
        ),
        grid=(2,),
        in_specs=[one, second, first, one, one, row],
        out_specs=(one, pl.BlockSpec((8, width), lambda i: (0, 0))),
        compiler_params=params(),
        name="in_back",
    )(x, a, b, c, dmid, gain)


def remote(src, dst, send, recv, dp, seq):
    return pltpu.make_async_remote_copy(
        src_ref=src,
        dst_ref=dst,
        send_sem=send,
        recv_sem=recv,
        device_id=(dp, seq),
        device_id_type=pl.DeviceIdType.MESH,
    )


def greet(peers):
    barrier = pltpu.get_barrier_semaphore()
    for dp, seq in peers:
        pl.semaphore_signal(
            barrier, inc=1, device_id=(dp, seq), device_id_type=pl.DeviceIdType.MESH
        )
    pl.semaphore_wait(barrier, len(peers))


class GradSum:
    def __init__(self, part, acc, landx, land, sems, dp, seq):
        self.part, self.landx, self.land, self.sems = part, landx, land, sems
        self.fetched = acc is not None
        self.acc = acc if self.fetched else landx
        self.seq, self.z, self.x = seq, dp // 2, dp % 2

    def cross(self, k):
        return remote(
            self.part.at[2 * k + (1 - self.x)],
            self.landx.at[k],
            self.sems.at[0, k],
            self.sems.at[1, k],
            2 * self.z + (1 - self.x),
            self.seq,
        )

    def fetch(self, k):
        return pltpu.make_async_copy(
            self.part.at[2 * k + self.x], self.acc.at[k], self.sems.at[6, k]
        )

    def right(self, b, first):
        return remote(
            self.acc.at[b] if first else self.land.at[b + 1],
            self.land.at[b + 1],
            self.sems.at[2, b],
            self.sems.at[3, b],
            2 * ((self.z + 1) % 4) + self.x,
            self.seq,
        )

    def left(self, b, first):
        return remote(
            self.acc.at[b] if first else self.land.at[b],
            self.land.at[b],
            self.sems.at[4, b],
            self.sems.at[5, b],
            2 * ((self.z + 3) % 4) + self.x,
            self.seq,
        )

    def start(self):
        for k in (3, 0, 2, 1):
            self.cross(k).start()
        if self.fetched:
            for k in range(4):
                self.fetch(k).start()

    def add_cross(self):
        for k in (3, 0, 2, 1):
            self.cross(k).wait_recv()
            if self.fetched:
                self.fetch(k).wait()
                own = self.acc[k].astype(f32)
            else:
                own = self.part[2 * k + self.x].astype(f32)
            self.acc[k] = (own + self.landx[k].astype(f32)).astype(bf16)

    def stage(self, k):
        @pl.when(self.z == k)
        def _():
            for b in range(3, k, -1):
                if k > 0:
                    self.right(b, False).wait_recv()
                    total = self.land[b + 1].astype(f32) + self.acc[b].astype(f32)
                    self.land[b + 1] = total.astype(bf16)
                self.right(b, k == 0).start()

        @pl.when(self.z == 3 - k)
        def _():
            for b in range(0, 3 - k):
                if k > 0:
                    self.left(b, False).wait_recv()
                    total = self.land[b].astype(f32) + self.acc[b].astype(f32)
                    self.land[b] = total.astype(bf16)
                self.left(b, k == 0).start()

    def finish(self, out):
        z = self.z
        out[...] = self.acc[z].astype(f32)

        @pl.when(z > 0)
        def _():
            self.right(z, False).wait_recv()
            out[...] += self.land[z + 1].astype(f32)

        @pl.when(z < 3)
        def _():
            self.left(z, False).wait_recv()
            out[...] += self.land[z].astype(f32)

    def drain(self):
        for k in range(4):
            self.cross(k).wait_send()
        for k in range(3):

            @pl.when(self.z == k)
            def _(k=k):
                for b in range(3, k, -1):
                    self.right(b, k == 0).wait_send()

            @pl.when(self.z == 3 - k)
            def _(k=k):
                for b in range(0, 3 - k):
                    self.left(b, k == 0).wait_send()

    @staticmethod
    def scratch(m, n, fetched=False):
        own = [pltpu.VMEM((4, m, n), bf16)] if fetched else []
        return own + [
            pltpu.VMEM((4, m, n), bf16),
            pltpu.VMEM((5, m, n), bf16),
            pltpu.SemaphoreType.DMA((7, 4)),
        ]


SMALL_ROWS = 16


class Gather:
    def __init__(self, own, slot, sems, dp, seq):
        self.own, self.slot, self.sems = own, slot, sems
        self.dp, self.seq, self.z, self.x = dp, seq, dp // 2, dp % 2

    def along(self, k, step, src=None):
        slot = self.slot(2 * k + self.x)
        return remote(
            slot if src is None else src,
            slot,
            self.sems.at[0 if step > 0 else 1, k],
            self.sems.at[3, k],
            2 * ((self.z + step + 4) % 4) + self.x,
            self.seq,
        )

    def over(self, k, src=None):
        slot = self.slot(2 * k + self.x)
        return remote(
            slot if src is None else src,
            slot,
            self.sems.at[2, k],
            self.sems.at[4, k],
            2 * self.z + (1 - self.x),
            self.seq,
        )

    def keep(self):
        return pltpu.make_async_copy(self.own, self.slot(self.dp), self.sems.at[5, 0])

    def start(self):
        z = self.z

        @pl.when(z < 3)
        def _():
            self.along(z, 1, self.own).start()

        @pl.when(z > 0)
        def _():
            self.along(z, -1, self.own).start()

        self.over(z, self.own).start()
        self.keep().start()

    def hop(self, dist):
        z = self.z

        @pl.when(z - dist >= 0)
        def _():
            k = z - dist
            self.along(k, 1).wait_recv()

            @pl.when(z < 3)
            def _():
                self.along(k, 1).start()

            self.over(k).start()

        @pl.when(z + dist <= 3)
        def _():
            k = z + dist
            self.along(k, -1).wait_recv()

            @pl.when(z > 0)
            def _():
                self.along(k, -1).start()

            self.over(k).start()

    def arrive(self):
        self.keep().wait()
        for k in range(4):
            self.over(k).wait_recv()

    def drain(self):
        z = self.z
        for k in range(4):
            self.over(k).wait_send()

            @pl.when((z < 3) & (z >= k))
            def _(k=k):
                self.along(k, 1).wait_send()

            @pl.when((z > 0) & (z <= k))
            def _(k=k):
                self.along(k, -1).wait_send()

    @staticmethod
    def scratch():
        return pltpu.SemaphoreType.DMA((6, 4))


class Spread:
    def __init__(self, own, rows, sems, dp, seq):
        mate, across = seq + 1 - 2 * (seq % 2), (seq + 2) % 4
        to = lambda src, r, peer: remote(src, rows.at[r], sems.at[0, r], sems.at[1, r], dp, peer)
        self.near, self.far = to(own, 1, mate), to(own, 2, across)
        self.last = to(rows.at[2], 3, mate)

    def start(self):
        self.far.start()
        self.near.start()

    def forward(self):
        self.far.wait_recv()
        self.last.start()

    def drain(self):
        for copy in (self.near, self.far, self.last):
            copy.wait_send()


def neighbours(seq):
    mate = seq + 1 - 2 * (seq % 2)
    return mate, (seq + 2) % 4, (mate + 2) % 4


def block_at(seq, rel):
    return 2 * ((seq // 2 + rel // 2) % 2) + (seq + rel) % 2


def scores(k, qm, ramp):
    block = qm.shape[0]
    length = k.shape[0]
    s = mm_t(k, qm) + jnp.concatenate([ramp] * (block // LANES), axis=1)
    key = lax.broadcasted_iota(jnp.int32, (block, block), 0)
    query = lax.broadcasted_iota(jnp.int32, (block, block), 1)
    last = jnp.where(key <= query, s[length - block :], NEG)
    if length == block:
        return last
    return jnp.concatenate([s[: length - block], last], axis=0)


def fore_body(
    scal, slopes, wq, wo, x, v_up, v_qv, v_g1, v_s1, v_out, v_g2, v_s2, v_down, g, w1, w2,
    h1, qkv_out, o, lse, wq_all, flat, mid, gain1, bias_down, y_all, gw1, gw2, dmid, dbr, sums,
    up_sum,
    small, vectors, shift1, bias_qkv, bias_out, gain2, shift2, bias_up,
    rows_in, g_rows, h_stage, qkv, ramp, vt, part, land_c, sum_y, land_y, w1_all, w2_flat,
    a_all, du_all, turned, y_stage, up_stage, down_stage,
    q_sem, o_sem, w1_sem, w2_sem, x_sem, g_sem, seq_sem, dp_sem, keep_sem, stage_sem, fwd, mlp, bwd,
):
    dp, seq = lax.axis_index("dp"), lax.axis_index("seq")
    mate, across, _ = neighbours(seq)
    greet([((dp + i) % 8, seq) for i in range(1, 8)] + [(dp, p) for p in neighbours(seq)])
    rows, width = x.shape
    keys = qkv.shape[0]
    inner = o.shape[1]
    pairs = inner // LANES
    ff = du_all.shape[1]
    half_rows = rows // 2
    halves = [slice(0, half_rows), slice(half_rows, rows)]
    column = lambda ref: lambda d: ref.at[:, pl.ds(pl.multiple_of(d * LANES, LANES), LANES)]

    gather_q = Gather(wq, lambda d: wq_all.at[d], q_sem, dp, seq)
    gather_o = Gather(wo, column(flat), o_sem, dp, seq)
    gathers = [
        Gather(w1, lambda d: w1_all.at[d], w1_sem, dp, seq),
        Gather(w2, column(w2_flat), w2_sem, dp, seq),
    ]
    spread_x = Spread(x, rows_in, x_sem, dp, seq)
    spread_g = Spread(g, g_rows, g_sem, dp, seq)
    at = 0
    for ref in (v_up, v_qv, v_g1, v_s1, v_out, v_g2, v_s2, v_down):
        small[:, at : at + ref.shape[1]] = ref[...].astype(f32)
        at += ref.shape[1]
    keep_v = pltpu.make_async_copy(small, vectors.at[dp, seq], keep_sem.at[0])
    keep_v.start()
    group = [
        remote(small, vectors.at[dp, seq], seq_sem.at[0, i], seq_sem.at[1, i], dp, peer)
        for i, peer in enumerate(neighbours(seq))
    ]
    for copy in group:
        copy.start()
    gather_q.start()
    spread_x.start()
    keep_x = pltpu.make_async_copy(x, rows_in.at[0], keep_sem.at[1])
    keep_g = pltpu.make_async_copy(g, g_rows.at[0], keep_sem.at[2])
    keep_x.start()
    keep_g.start()

    def to_dp(i):
        return remote(
            vectors.at[dp], vectors.at[dp], dp_sem.at[0, i], dp_sem.at[1, i], (dp + i) % 8, seq
        )

    keep_v.wait()
    for copy in group:
        copy.wait_recv()
    for i in range(1, 8):
        to_dp(i).start()
    gather_o.start()
    spread_g.start()
    gather_q.hop(1)
    gather_q.hop(2)
    gather_o.hop(1)
    gather_q.hop(3)
    gather_o.hop(2)
    spread_x.forward()
    gather_o.hop(3)
    for gather in gathers:
        gather.start()
    for i in range(1, 8):
        to_dp(i).wait_recv()
    for ref, at in (
        (gain1, 192), (shift1, 224), (bias_out, 256), (gain2, 288), (shift2, 320), (bias_down, 352),
    ):
        for d in range(8):
            ref[:, d * LANES : (d + 1) * LANES] = jnp.concatenate(
                [vectors[d, i, :, at : at + 32] for i in range(4)], axis=1
            )
    for section in range(2):
        for half in range(2):
            lane = section * 512 + half * LANES
            bias_qkv[:, lane : lane + LANES] = jnp.concatenate(
                [vectors[4 * section + seq, 2 * half + i, :, 128:192] for i in range(2)], axis=1
            )
    bias_qkv[:, 256:512] = jnp.zeros((1, 256), f32)
    for i in range(8):
        bias_up[:, i * LANES : (i + 1) * LANES] = vectors[2 * seq + i // 4, i % 4, :, 0:LANES]
    keep_x.wait()
    spread_x.near.wait_recv()
    gather_q.arrive()
    spread_x.last.wait_recv()
    spread_x.drain()

    def h1_copy(r):
        at = pl.ds(pl.multiple_of(block_at(seq, r) * rows, rows), rows)
        return pltpu.make_async_copy(h_stage.at[r % 2], h1.at[at], stage_sem.at[0, r % 2])

    def project(r, carry):
        @pl.when(r >= 2)
        def _():
            h1_copy(r - 2).wait()

        at = pl.ds(pl.multiple_of(block_at(seq, r) * rows, rows), rows)
        unit, _ = normalize(rows_in[r].astype(f32))
        low = (unit * gain1[...] + shift1[...]).astype(bf16)
        h_stage[r % 2] = low
        h1_copy(r).start()
        weight = wq_all[...].reshape(width, 3 * inner)
        qkv[at, :] = (mm(low, weight) + bias_qkv[...]).astype(bf16)
        return carry

    lax.fori_loop(0, 4, project, 0)
    qkv_copy = pltpu.make_async_copy(qkv, qkv_out, keep_sem.at[3])
    qkv_copy.start()
    for gather in gathers:
        gather.hop(1)
    spread_g.forward()
    pos = lax.broadcasted_iota(jnp.int32, (keys, LANES), 0)
    ramp[...] = jnp.where(pos < scal[1], pos.astype(f32), -1e33)
    for p in range(pairs):
        vt[p] = qkv[:, 2 * inner + p * LANES : 2 * inner + (p + 1) * LANES].T
    gather_o.arrive()

    def row_copies(sems):
        rel_one = remote(part.at[1], land_c.at[0], sems.at[0, 0], sems.at[1, 0], dp, mate)
        rel_three = [
            remote(
                part.at[3, at], land_c.at[1, at], sems.at[0, 1 + i], sems.at[1, 1 + i], dp, mate
            )
            for i, at in enumerate(halves)
        ]
        over = [
            remote(sum_y.at[at], land_y.at[at], sems.at[0, 3 + i], sems.at[1, 3 + i], dp, across)
            for i, at in enumerate(halves)
        ]
        return rel_one, rel_three, over

    def send_over(rel_three, over, i):
        rel_three[i].wait_recv()
        at = halves[i]
        total = part[2, at, :].astype(f32) + land_c[1, at, :].astype(f32)
        sum_y[at, :] = total.astype(bf16)
        over[i].start()

    rel_one, rel_three, over = row_copies(fwd)

    def attend(t, carry):
        rel = 3 - t
        c_now = block_at(seq, rel)
        at = pl.ds(pl.multiple_of(c_now * rows, rows), rows)
        for c in range(keys // rows):

            @pl.when(c_now == c)
            def _(c=c):
                length = (c + 1) * rows

                def one_pair(p, carry):
                    lane = pl.ds(pl.multiple_of(p * LANES, LANES), LANES)
                    k_lane = pl.ds(pl.multiple_of(inner + p * LANES, LANES), LANES)
                    scaled = qkv[c * rows : length, lane] * bf16(HEAD_DIM**-0.5)
                    k = qkv[0:length, k_lane]
                    outs, logs = [], []
                    for h in range(2):
                        bias = ramp[0:length, :] * slopes[2 * p + h]
                        s = scores(k, head_only(scaled, h), bias)
                        top = jnp.max(s, axis=0, keepdims=True)
                        e = jnp.exp(s - top)
                        total = jnp.sum(e, axis=0, keepdims=True)
                        half = vt[p, h * HEAD_DIM : (h + 1) * HEAD_DIM, 0:length]
                        outs.append(mm(half, e.astype(bf16)) / total)
                        logs.append(top + jnp.log(total))
                    o[c * rows : length, lane] = jnp.concatenate(outs, axis=0).T.astype(bf16)
                    lse[p, 0:2, c * rows : length] = jnp.concatenate(logs, axis=0)
                    return carry

                lax.fori_loop(0, pairs, one_pair, 0)

        part[rel] = mm(o[at, :], flat[...]).astype(bf16)

        @pl.when(t == 0)
        def _():
            for copy in rel_three:
                copy.start()

        @pl.when(t == 1)
        def _():
            send_over(rel_three, over, 0)
            send_over(rel_three, over, 1)
            for gather in gathers:
                gather.hop(2)

        @pl.when(t == 2)
        def _():
            rel_one.start()
            for gather in gathers:
                gather.hop(3)

        return carry

    lax.fori_loop(0, 4, attend, 0)
    gather_q.drain()
    gather_o.drain()
    rel_one.wait_recv()

    near, far, last = (
        [
            remote(
                rows_in.at[0 if r < 3 else 2, at], rows_in.at[r, at], mlp.at[0, 2 * k + i],
                mlp.at[1, 2 * k + i], dp, across if r == 2 else mate,
            )
            for i, at in enumerate(halves)
        ]
        for k, r in enumerate((1, 2, 3))
    )
    step_rows = 64

    def second_norm(i):
        over[i].wait_recv()

        def step(k, carry):
            at = pl.ds(pl.multiple_of(i * half_rows + k * step_rows, step_rows), step_rows)
            total = (part[0, at, :].astype(f32) + land_c[0, at, :].astype(f32)) + land_y[
                at, :
            ].astype(f32)
            value = rows_in[0, at, :].astype(f32) + (total + bias_out[...])
            mid[at, :] = value
            unit, _ = normalize(value)
            rows_in[0, at, :] = (unit * gain2[...] + shift2[...]).astype(bf16)
            return carry

        lax.fori_loop(0, half_rows // step_rows, step, 0)
        far[i].start()
        near[i].start()

    second_norm(0)
    up_sum[...] = jnp.zeros_like(up_sum)
    sums[...] = jnp.zeros_like(sums)
    keep_g.wait()
    spread_g.near.wait_recv()
    spread_g.last.wait_recv()
    spread_g.drain()
    for gather in gathers:
        gather.arrive()
    for copy in [rel_one] + rel_three:
        copy.wait_send()
    back_one, back_three, back_over = row_copies(bwd)
    chunk = 256

    def y_copy(i):
        rel, half = place(i)
        at = pl.ds(pl.multiple_of(half * half_rows, half_rows), half_rows)
        return pltpu.make_async_copy(y_stage.at[i % 2], y_all.at[rel, at], stage_sem.at[1, i % 2])

    def place(i):
        late = i // 4
        return late * (2 + i % 2) + (1 - late) * (i // 2), late * ((i // 2) % 2) + (1 - late) * (i % 2)

    def block(i, carry):
        rel, half = place(i)

        @pl.when(i == 1)
        def _():
            second_norm(1)

        for k in range(2):

            @pl.when(i == 2 + k)
            def _(k=k):
                near[k].wait_recv()

            @pl.when(i == 4 + 2 * k)
            def _(k=k):
                far[k].wait_recv()
                last[k].start()

            @pl.when(i == 5 + 2 * k)
            def _(k=k):
                last[k].wait_recv()

        @pl.when(i >= 2)
        def _():
            y_copy(i - 2).wait()

        inside = pl.ds(pl.multiple_of(half * half_rows, half_rows), half_rows)
        at = pl.ds(pl.multiple_of(rel * rows + half * half_rows, half_rows), half_rows)
        hidden = rows_in[rel, inside, :]
        grad = g_rows[rel, inside, :]
        up = w1_all[...].reshape(width, ff)
        for c in range(ff // chunk):
            cols = slice(c * chunk, (c + 1) * chunk)
            u = mm(hidden, up[:, cols]) + bias_up[:, cols]
            value, slope = gelu_parts(u)
            a_all[at, cols] = value.astype(bf16)
            du = (mm_t(grad, w2_flat[cols, :]) * slope).astype(bf16)
            du_all[at, cols] = du
            up_sum[:, cols] += jnp.sum(du.astype(f32), axis=0, keepdims=True)
        y_stage[i % 2] = mm(a_all[at, :], w2_flat[...]).astype(bf16)
        y_copy(i).start()
        part[rel, inside, :] = mm_t(du_all[at, :], up).astype(bf16)

        @pl.when(i == 3)
        def _():
            back_one.start()

        @pl.when(i == 5)
        def _():
            back_three[0].start()

        @pl.when(i == 6)
        def _():
            over[0].wait_send()
            over[1].wait_send()
            send_over(back_three, back_over, 0)

        @pl.when(i == 7)
        def _():
            back_three[1].start()

        return carry

    lax.fori_loop(0, 8, block, 0)

    def turn(load):
        def step(i, carry):
            turned[:, pl.ds(pl.multiple_of(i * rows, rows), rows)] = load(i).T
            return carry

        lax.fori_loop(0, 4, step, 0)

    def up_copy(j):
        cols = pl.ds(pl.multiple_of(j * chunk, chunk), chunk)
        return pltpu.make_async_copy(up_stage.at[j % 2], gw1.at[:, :, cols], stage_sem.at[2, j % 2])

    def down_copy(j):
        return pltpu.make_async_copy(
            down_stage.at[j % 2], gw2.at[pl.ds(2 * j, 2)], stage_sem.at[3, j % 2]
        )

    def outer_up(j, carry):
        @pl.when(j >= 2)
        def _():
            up_copy(j - 2).wait()

        cols = pl.ds(pl.multiple_of(j * chunk, chunk), chunk)
        value = mm(turned[...], du_all[:, cols]).astype(bf16)
        up_stage[j % 2] = value.reshape(8, width // 8, chunk)
        up_copy(j).start()
        return carry

    def outer_down(j, carry):
        @pl.when(j >= 2)
        def _():
            down_copy(j - 2).wait()

        cols = pl.ds(pl.multiple_of(j * chunk, chunk), chunk)
        right = g_rows[:, :, cols].reshape(4 * rows, chunk)
        value = mm(turned[...], right).astype(bf16)
        down_stage[j % 2, 0] = value[:, :LANES]
        down_stage[j % 2, 1] = value[:, LANES:]
        down_copy(j).start()
        return carry

    turn(lambda i: rows_in[i])
    send_over(back_three, back_over, 1)
    lax.fori_loop(0, ff // chunk, outer_up, 0)
    turn(lambda i: a_all[pl.ds(pl.multiple_of(i * rows, rows), rows), :])
    lax.fori_loop(0, width // chunk, outer_down, 0)

    back_one.wait_recv()

    def norm_step(k, carry):
        at = pl.ds(pl.multiple_of(k * step_rows, step_rows), step_rows)
        unit, inv = normalize(mid[at, :])
        e = (part[0, at, :].astype(f32) + land_c[0, at, :].astype(f32)) + land_y[at, :].astype(f32)
        grad = g_rows[0, at, :].astype(f32)
        value = grad + norm_back(e, gain2[...], unit, inv)
        dmid[at, :] = value
        low = value.astype(bf16)
        dbr[at, :] = low
        sums[0:1, :] += jnp.sum(e * unit, axis=0, keepdims=True)
        sums[1:2, :] += jnp.sum(e, axis=0, keepdims=True)
        sums[2:3, :] += jnp.sum(low.astype(f32), axis=0, keepdims=True)
        sums[3:4, :] += jnp.sum(grad, axis=0, keepdims=True)
        return carry

    steps = half_rows // step_rows
    back_over[0].wait_recv()
    lax.fori_loop(0, steps, norm_step, 0)
    back_over[1].wait_recv()
    lax.fori_loop(steps, 2 * steps, norm_step, 0)

    for copy in group + near + far + last + [back_one] + back_three + back_over:
        copy.wait_send()
    for i in range(1, 8):
        to_dp(i).wait_send()
    for gather in gathers:
        gather.drain()
    qkv_copy.wait()
    for k in range(2):
        h1_copy(2 + k).wait()
        y_copy(6 + k).wait()
        up_copy(ff // chunk - 2 + k).wait()
        down_copy(width // chunk - 2 + k).wait()


def fore_call(scal, slopes, wq, wo, x, small, g, w1, w2):
    rows, width = x.shape
    keys = 4 * rows
    inner, ff = wo.shape[0], w1.shape[1]
    pairs = inner // LANES
    count = sum(v.shape[0] for v in small)
    sem = pltpu.SemaphoreType.DMA
    shape = jax.ShapeDtypeStruct
    any_space = pl.BlockSpec(memory_space=pl.ANY)
    vec = lambda n: pltpu.VMEM((1, n), f32)
    block = lambda *lead: pltpu.VMEM((*lead, rows, width), bf16)
    return pl.pallas_call(
        fore_body,
        out_shape=(
            shape((keys, width), bf16),
            shape((keys, 3 * inner), bf16),
            shape((keys, inner), bf16),
            shape((pairs, 8, keys), f32),
            shape((8, *wq.shape), bf16),
            shape((inner, width), bf16),
            shape((rows, width), f32),
            shape((1, width), f32),
            shape((1, width), f32),
            shape((4, rows, width), bf16),
            shape((8, width // 8, ff), bf16),
            shape((8, ff, LANES), bf16),
            shape((rows, width), f32),
            shape((rows, width), bf16),
            shape((8, width), f32),
            shape((1, ff), f32),
        ),
        in_specs=[SCALAR, SCALAR] + [any_space] * 3 + [WHOLE] * 8 + [any_space] * 3,
        out_specs=(
            any_space, any_space, WHOLE, WHOLE, WHOLE, WHOLE, WHOLE, WHOLE, WHOLE,
            any_space, any_space, any_space, WHOLE, WHOLE, WHOLE, WHOLE,
        ),
        scratch_shapes=[
            vec(count),
            pltpu.VMEM((8, 4, 1, count), f32),
            vec(width), vec(3 * inner), vec(width), vec(width), vec(width), vec(ff),
            block(4),
            block(4),
            block(2),
            pltpu.VMEM((keys, 3 * inner), bf16),
            pltpu.VMEM((keys, LANES), f32),
            pltpu.VMEM((pairs, LANES, keys), bf16),
            block(4),
            block(2),
            block(),
            block(),
            pltpu.VMEM((8, *w1.shape), bf16),
            pltpu.VMEM((ff, width), bf16),
            pltpu.VMEM((keys, ff), bf16),
            pltpu.VMEM((keys, ff), bf16),
            pltpu.VMEM((width, keys), bf16),
            pltpu.VMEM((2, rows // 2, width), bf16),
            pltpu.VMEM((2, 8, width // 8, 256), bf16),
            pltpu.VMEM((2, 2, ff, LANES), bf16),
            Gather.scratch(), Gather.scratch(), Gather.scratch(), Gather.scratch(),
            sem((2, 4)), sem((2, 4)), sem((2, 3)), sem((2, 8)), sem((4,)), sem((4, 2)),
            sem((2, 5)), sem((2, 6)), sem((2, 5)),
        ],
        compiler_params=pltpu.CompilerParams(
            vmem_limit_bytes=67043328, collective_id=4, has_side_effects=True
        ),
        name="fore",
    )(scal, slopes, wq, wo, x, *(v.reshape(1, -1) for v in small), g, w1, w2)


def back_body(
    scal, slopes, dbr, o, flat, qkv, lse, wq, h1, gw1, gw2, y_all, mid, bias_down, x, dmid,
    gain1, mid_sums, up_sum,
    output, grad, gq_out, go_out, gw1_out, gw2_out, small_out,
    b_rows, y_far, do, go_sum, go_part, bias, kt, dk_sum, dv_sum, merged, qkv_sums, h_buf, turned,
    gq_part, land_c, sum_y, land_y, y_land_c, y_sum, y_land_y,
    a_acc, a_x, a_land, a_sem, b_acc, b_x, b_land, b_sem, o_x, o_land, o_sem,
    q0_x, q0_land, q0_sem, q1_x, q1_land, q1_sem, q2_x, q2_land, q2_sem,
    small, small_land, own, seq_land,
    b_row_sem, row_sems, y_sems, h_sem, small_sems, seq_sems, far_sem,
):
    dp, seq = lax.axis_index("dp"), lax.axis_index("seq")
    mate, across, far_mate = neighbours(seq)
    greet([((dp + i) % 8, seq) for i in range(1, 8)] + [(dp, p) for p in neighbours(seq)])
    rows, width = dbr.shape
    keys, inner = o.shape
    pairs = inner // LANES
    scale = HEAD_DIM**-0.5
    chunk = 128

    spread_b = Spread(dbr, b_rows, b_row_sem, dp, seq)
    spread_b.start()
    sum_a = GradSum(gw2, a_acc, a_x, a_land, a_sem, dp, seq)
    sum_b = GradSum(gw1, b_acc, b_x, b_land, b_sem, dp, seq)
    sum_o = GradSum(go_part, None, o_x, o_land, o_sem, dp, seq)
    sums_q = [
        GradSum(gq_part.at[0], None, q0_x, q0_land, q0_sem, dp, seq),
        GradSum(gq_part.at[1], None, q1_x, q1_land, q1_sem, dp, seq),
        GradSum(gq_part.at[2], None, q2_x, q2_land, q2_sem, dp, seq),
    ]
    sum_a.start()
    sum_b.start()
    y_cores = [
        remote(y_all.at[1 + 2 * k], y_land_c.at[k], y_sems.at[0, k], y_sems.at[1, k], dp, mate)
        for k in range(2)
    ]
    y_over = remote(y_sum, y_land_y, y_sems.at[0, 2], y_sems.at[1, 2], dp, across)
    cores = [
        remote(b_rows.at[r], land_c.at[k], row_sems.at[0, k], row_sems.at[1, k], dp, mate)
        for k, r in ((0, 1), (1, 3))
    ]
    over = remote(sum_y, land_y, row_sems.at[0, 2], row_sems.at[1, 2], dp, across)

    def fetch_h(i):
        at = pl.ds(pl.multiple_of(i * rows, rows), rows)
        return pltpu.make_async_copy(h1.at[at], h_buf.at[i % 2], h_sem.at[i % 2])

    fetch_h(0).start()
    fetch_h(1).start()
    y_fetch = [
        pltpu.make_async_copy(y_all.at[2 - 2 * k], y_far.at[k], far_sem.at[k]) for k in range(2)
    ]
    for copy in y_fetch:
        copy.start()
    go_sum[...] = jnp.zeros_like(go_sum)

    def out_back(r, carry):
        if r >= 2:
            spread_b.forward() if r == 2 else spread_b.last.wait_recv()
        if r == 1:
            spread_b.near.wait_recv()
        at = pl.ds(pl.multiple_of(block_at(seq, r) * rows, rows), rows)
        src = dbr if r == 0 else b_rows.at[r]
        do[at, :] = mm_t(src[...], flat[...]).astype(bf16)
        go_sum[...] += mm(o[at, :].T, src[...])
        return carry

    out_back(0, 0)
    y_cores[1].start()
    y_cores[0].start()
    out_back(1, 0)

    def turn(i, carry):
        fetch_h(i).wait()
        turned[:, pl.ds(pl.multiple_of(i * rows, rows), rows)] = h_buf[i % 2].T

        @pl.when(i < 2)
        def _():
            fetch_h(i + 2).start()

        return carry

    lax.fori_loop(0, 4, turn, 0)
    small[...] = jnp.zeros_like(small)
    for d in range(8):
        at = slice(d * LANES, (d + 1) * LANES)
        for row, src in ((4, 2), (5, 0), (6, 1), (11, 3)):
            small[d, row : row + 1, :] = mid_sums[src : src + 1, at]
    for i in range(8):
        at = slice(i * LANES, (i + 1) * LANES)
        small[pl.ds(2 * seq + i // 4, 1), 7 + i % 4, :] = up_sum[:, at]
    out_back(2, 0)
    y_cores[1].wait_recv()
    for copy in y_fetch:
        copy.wait()
    for i in range(rows // chunk):
        at = slice(i * chunk, (i + 1) * chunk)
        total = y_far[0, at, :].astype(f32) + y_land_c[1, at, :].astype(f32)
        y_sum[at, :] = total.astype(bf16)
    y_over.start()
    out_back(3, 0)
    for d in range(8):
        go_part[d] = go_sum[:, d * LANES : (d + 1) * LANES].astype(bf16)
    sum_o.start()
    sum_a.add_cross()
    sum_a.stage(0)

    def one_pair(p, carry):
        lane = pl.ds(pl.multiple_of(p * LANES, LANES), LANES)
        k_lane = pl.ds(pl.multiple_of(inner + p * LANES, LANES), LANES)
        v_lane = pl.ds(pl.multiple_of(2 * inner + p * LANES, LANES), LANES)
        pos = lax.broadcasted_iota(jnp.int32, (keys, LANES), 0)
        ramp = pos.astype(f32)
        inside = pos < scal[1]
        for h in range(2):
            bias[h] = jnp.where(inside, ramp * slopes[2 * p + h], NEG)
        kt[...] = qkv[:, k_lane].T
        dk_sum[...] = jnp.zeros_like(dk_sum)
        dv_sum[...] = jnp.zeros_like(dv_sum)
        for c in range(keys // rows):
            length = (c + 1) * rows
            at = slice(c * rows, length)
            scaled = qkv[at, lane] * bf16(scale)
            g = do[at, lane]
            both = (g.astype(f32) * o[at, lane].astype(f32)).T
            k = qkv[0:length, k_lane]
            v = qkv[0:length, v_lane]
            outs = []
            for h in range(2):
                half = slice(h * HEAD_DIM, (h + 1) * HEAD_DIM)
                qm = head_only(scaled, h)
                gm = head_only(g, h)
                dot_row = jnp.sum(both[half], axis=0, keepdims=True)
                log = lse[p, h : h + 1, at]
                e = jnp.exp(scores(k, qm, bias[h, 0:length, :]) - log)
                ds = (e * (mm_t(v, gm) - dot_row)).astype(bf16)
                dv_sum[0:length, :] += mm(e.astype(bf16), gm)
                dk_sum[0:length, :] += mm(ds, qm)
                outs.append(mm(kt[half, 0:length], ds))
            merged[at, lane] = (jnp.concatenate(outs, axis=0).T * scale).astype(bf16)
            if c == 2:

                @pl.when(p == 1)
                def _():
                    sum_a.stage(2)

        merged[:, k_lane] = dk_sum[...].astype(bf16)
        merged[:, v_lane] = dv_sum[...].astype(bf16)

        @pl.when(p == 0)
        def _():
            sum_a.stage(1)

        return carry

    lax.fori_loop(0, pairs, one_pair, 0)
    spread_b.drain()
    sum_b.add_cross()
    sum_b.stage(0)
    qkv_sums[...] = jnp.zeros_like(qkv_sums)

    def qkv_back(t, carry):
        rel = 3 - t
        at = pl.ds(pl.multiple_of(block_at(seq, rel) * rows, rows), rows)
        low = merged[at, :]
        b_rows[rel] = mm_t(low, wq[...]).astype(bf16)
        qkv_sums[...] += jnp.sum(low.astype(f32), axis=0, keepdims=True)

        @pl.when(t == 0)
        def _():
            cores[1].start()

        @pl.when(t == 1)
        def _():
            cores[1].wait_recv()
            for i in range(rows // chunk):
                at = slice(i * chunk, (i + 1) * chunk)
                total = b_rows[2, at, :].astype(f32) + land_c[1, at, :].astype(f32)
                sum_y[at, :] = total.astype(bf16)
            over.start()

        @pl.when(t == 2)
        def _():
            cores[0].start()

        return carry

    lax.fori_loop(0, 4, qkv_back, 0)
    for j in range(3):
        cols = slice(j * inner, (j + 1) * inner)
        value = mm(turned[...], merged[:, cols]).astype(bf16)
        gq_part[j] = value.reshape(8, width // 8, inner)
        sums_q[j].start()
        if j == 0:
            sum_o.add_cross()
            sum_o.stage(0)
            sum_b.stage(1)
    for i in range(2):
        at = slice(i * LANES, (i + 1) * LANES)
        small[pl.ds(seq, 1), 2 + i, :] = qkv_sums[:, at]
        at = slice((4 + i) * LANES, (5 + i) * LANES)
        small[pl.ds(4 + seq, 1), 2 + i, :] = qkv_sums[:, at]
    sum_a.finish(gw2_out)
    y_cores[0].wait_recv()
    y_over.wait_recv()

    def out_step(i, carry):
        at = pl.ds(pl.multiple_of(i * chunk, chunk), chunk)
        total = y_far[1, at, :].astype(f32) + y_land_c[0, at, :].astype(f32)
        total = total + y_land_y[at, :].astype(f32)
        output[at, :] = (mid[at, :] + (total + bias_down[...])).astype(bf16)
        return carry

    lax.fori_loop(0, rows // chunk, out_step, 0)
    sums_q[0].add_cross()
    sums_q[0].stage(0)
    sum_b.stage(2)
    sum_o.stage(1)
    cores[0].wait_recv()
    over.wait_recv()
    own[...] = jnp.zeros_like(own)
    qkv_gain = [jnp.zeros((1, width), f32), jnp.zeros((1, width), f32)]
    for i in range(rows // chunk):
        at = slice(i * chunk, (i + 1) * chunk)
        unit, inv = normalize(x[at, :].astype(f32))
        e = (b_rows[0, at, :].astype(f32) + land_c[0, at, :].astype(f32)) + land_y[
            at, :
        ].astype(f32)
        grad[at, :] = (dmid[at, :] + norm_back(e, gain1[...], unit, inv)).astype(bf16)
        qkv_gain[0] += jnp.sum(e * unit, axis=0, keepdims=True)
        qkv_gain[1] += jnp.sum(e, axis=0, keepdims=True)
    for d in range(8):
        at = slice(d * LANES, (d + 1) * LANES)
        small[d, 0:1, :] = qkv_gain[0][:, at]
        small[d, 1:2, :] = qkv_gain[1][:, at]

    def small_to(i):
        peer = (dp + i) % 8
        return remote(
            small.at[peer], small_land.at[i], small_sems.at[0, i], small_sems.at[1, i], peer, seq
        )

    for i in range(1, 8):
        small_to(i).start()
    sums_q[1].add_cross()
    sums_q[1].stage(0)
    sums_q[0].stage(1)
    sum_o.stage(2)
    sums_q[2].add_cross()
    sums_q[2].stage(0)
    sums_q[1].stage(1)
    sums_q[0].stage(2)
    total = small[dp]
    for i in range(1, 8):
        small_to(i).wait_recv()
        total = total + small_land[i]
    own[...] = total

    def seq_to(i, peer):
        return remote(own, seq_land.at[i], seq_sems.at[0, i], seq_sems.at[1, i], dp, peer)

    group = [seq_to(i, peer) for i, peer in enumerate(neighbours(seq))]
    for copy in group:
        copy.start()
    sums_q[2].stage(1)
    sums_q[1].stage(2)
    sums_q[2].stage(2)
    sum_b.finish(gw1_out)
    sum_o.finish(go_out)
    for copy in group:
        copy.wait_recv()
    small_out[...] = (own[...] + seq_land[0]) + (seq_land[1] + seq_land[2])
    for j in range(3):
        sums_q[j].finish(gq_out.at[:, j * inner : (j + 1) * inner])
    for copy in group + cores + y_cores + [over, y_over]:
        copy.wait_send()
    for i in range(1, 8):
        small_to(i).wait_send()
    for part in [sum_a, sum_b, sum_o] + sums_q:
        part.drain()


def back_call(*args):
    dbr, o, wo, qkv, lse, wq, h1, gw1, gw2 = args[2:11]
    rows, width = dbr.shape
    keys, inner = o.shape
    sem = pltpu.SemaphoreType.DMA
    block = lambda dtype: pltpu.VMEM((rows, width), dtype)
    pair_rows = pltpu.VMEM((2, rows, width), bf16)
    any_space = pl.BlockSpec(memory_space=pl.ANY)
    specs = [SCALAR, SCALAR] + [WHOLE] * (len(args) - 2)
    for at in (8, 9, 10, 11):
        specs[at] = any_space
    shape = jax.ShapeDtypeStruct
    return pl.pallas_call(
        back_body,
        out_shape=(
            shape((rows, width), bf16),
            shape((rows, width), bf16),
            shape((width // 8, 3 * inner), f32),
            shape((inner, LANES), f32),
            shape(gw1.shape[1:], f32),
            shape(gw2.shape[1:], f32),
            shape((SMALL_ROWS, LANES), f32),
        ),
        in_specs=specs,
        out_specs=(WHOLE,) * 7,
        scratch_shapes=[
            pltpu.VMEM((4, rows, width), bf16),
            pair_rows,
            pltpu.VMEM((keys, inner), bf16),
            pltpu.VMEM((inner, width), f32),
            pltpu.VMEM((8, inner, LANES), bf16),
            pltpu.VMEM((2, keys, LANES), f32),
            pltpu.VMEM((LANES, keys), bf16),
            pltpu.VMEM((keys, LANES), f32),
            pltpu.VMEM((keys, LANES), f32),
            pltpu.VMEM((keys, 3 * inner), bf16),
            pltpu.VMEM((1, 3 * inner), f32),
            pair_rows,
            pltpu.VMEM((width, keys), bf16),
            pltpu.VMEM((3, 8, width // 8, inner), bf16),
            pair_rows, block(bf16), block(bf16),
            pair_rows, block(bf16), block(bf16),
            *GradSum.scratch(*gw2.shape[1:], fetched=True),
            *GradSum.scratch(*gw1.shape[1:], fetched=True),
            *GradSum.scratch(inner, LANES),
            *(GradSum.scratch(width // 8, inner) * 3),
            pltpu.VMEM((8, SMALL_ROWS, LANES), f32),
            pltpu.VMEM((8, SMALL_ROWS, LANES), f32),
            pltpu.VMEM((SMALL_ROWS, LANES), f32),
            pltpu.VMEM((3, SMALL_ROWS, LANES), f32),
            sem((2, 4)), sem((2, 3)), sem((2, 3)), sem((2,)), sem((2, 8)), sem((2, 3)), sem((2,)),
        ],
        compiler_params=pltpu.CompilerParams(
            vmem_limit_bytes=67043328, collective_id=3, has_side_effects=True
        ),
        name="back",
    )(*args)


def finish_body(
    scal, output, grad, gq, go, gw1, gw2, small,
    output_out, grad_out, gq_out, go_out, gw1_out, gw2_out,
    gain1, shift1, qv, bout, gain2, shift2, up, down,
):
    seq = scal[0]
    output_out[...] = output[...]
    grad_out[...] = grad[...]
    go_out[...] = go[...]
    gw1_out[...] = gw1[...]
    gw2_out[...] = gw2[...]
    cols = gq_out.shape[2]
    for c in range(3):
        gq_out[:, c, :] = gq[:, c * cols : (c + 1) * cols]
    for ref, row in ((gain1, 0), (shift1, 1), (bout, 4), (gain2, 5), (shift2, 6), (down, 11)):
        n = ref.shape[1]
        value = small[row : row + 1, 0:n]
        for i in range(1, 4):
            value = jnp.where(seq == i, small[row : row + 1, i * n : (i + 1) * n], value)
        ref[...] = value
    value = small[2:3, 0:64]
    for i in range(1, 4):
        at = 64 * (i % 2)
        value = jnp.where(seq == i, small[2 + i // 2 : 3 + i // 2, at : at + 64], value)
    qv[...] = value
    up[...] = small[pl.ds(7 + seq, 1), :]


def finish_call(scal, output, grad, gq, go, gw1, gw2, small):
    one = lambda n: jax.ShapeDtypeStruct((1, n), f32)
    like = lambda v: jax.ShapeDtypeStruct(v.shape, v.dtype)
    return pl.pallas_call(
        finish_body,
        out_shape=(
            like(output), like(grad),
            jax.ShapeDtypeStruct((gq.shape[0], 3, gq.shape[1] // 3), f32),
            like(go), like(gw1), like(gw2),
            one(32), one(32), one(64), one(32), one(32), one(32), one(LANES), one(32),
        ),
        in_specs=[SCALAR] + [WHOLE] * 7,
        out_specs=(WHOLE,) * 14,
        compiler_params=params(),
        name="finish",
    )(scal, output, grad, gq, go, gw1, gw2, small)


def after(value, *others):
    return lax.optimization_barrier((value, *others))[0]


def on_device(
    dp_n,
    seq_n,
    tokens,
    lengths,
    cotangent,
    ln1_gain,
    ln1_shift,
    w_qkv,
    b_qv,
    w_out,
    b_out,
    ln2_gain,
    ln2_shift,
    w_fc1,
    b_fc1,
    w_fc2,
    b_fc2,
):
    count = dp_n * seq_n
    rows, width = tokens.shape
    heads = width // HEAD_DIM
    inner = w_out.shape[0]
    ff = w_fc1.shape[1]
    s = lax.axis_index("seq")
    length = lengths[0]

    scal = jnp.stack([s.astype(jnp.int32), length])
    slopes = 2.0 ** (-8.0 * (jnp.arange(heads, dtype=jnp.int32) + 1).astype(f32) / heads)
    slopes = lax.dynamic_slice(slopes, (s * (heads // seq_n),), (heads // seq_n,))
    valid = s * rows + jnp.arange(rows, dtype=jnp.int32) < length
    grad_low = jnp.where(valid[:, None], cotangent, jnp.zeros_like(cotangent))
    wq_own = jnp.concatenate([w_qkv[:, c, :] for c in range(3)], axis=1)
    small = (ln1_gain, ln1_shift, b_qv, b_out, ln2_gain, ln2_shift, b_fc1, b_fc2)
    sizes = [v.shape[0] for v in small]
    ends = [sum(sizes[: i + 1]) for i in range(len(sizes))]
    block = 384
    fast = dp_n == 8 and seq_n == 4 and width == 8 * LANES and ff == width and inner == 2 * LANES
    if fast:
        parts = dp_n
        order = (b_fc1, b_qv, ln1_gain, ln1_shift, b_out, ln2_gain, ln2_shift, b_fc2)
        (
            h1, qkv, o, lse, wq, w_o, mid, gain1, bias_down, y_all, grad_up, grad_down, dmid, dbr,
            mid_sums, up_sum,
        ) = fore_call(scal, slopes, wq_own, w_out, tokens, order, grad_low, w_fc1, w_fc2)
        results = back_call(
            scal, slopes, dbr, o, w_o, qkv, lse, wq.reshape(width, 3 * inner), h1, grad_up,
            grad_down, y_all, mid, bias_down, tokens, dmid, gain1, mid_sums, up_sum,
        )
        output, grad_tokens, grad_qkv, grad_out, grad_up, grad_down, *vectors = finish_call(
            scal, *results
        )
        g_gain1, g_shift1, g_qv, g_bout, g_gain2, g_shift2, g_up, g_down = (
            v.reshape(n) for v, n in zip(vectors, sizes)
        )
        return (
            output, grad_tokens, g_gain1, g_shift1, grad_qkv, g_qv, grad_out, g_bout,
            g_gain2, g_shift2, grad_up, g_up, grad_down, g_down,
        )

    wq = lax.all_gather(wq_own, "dp", axis=0, tiled=True)
    col = w_fc2.shape[1]
    both = jnp.concatenate([w_fc2, w_out], axis=0)
    if col % LANES == 0:
        parts = dp_n
        w_cols = lax.all_gather(both, "dp", axis=0, tiled=False)
    else:
        parts = 1
        w_cols = lax.all_gather(both, "dp", axis=1, tiled=True)[None]
    w_o = w_cols
    out_first = ff
    w1 = lax.all_gather(w_fc1, "dp", axis=0, tiled=True)
    packed = small_gather(jnp.concatenate([v.astype(f32) for v in small]), count, seq_n)
    packed = packed.reshape(count, ends[-1])
    gain1, shift1, bias_qv, bias_out, gain2, shift2, bias_up, bias_down = (
        packed[:, e - n : e].reshape(1, count * n) for e, n in zip(ends, sizes)
    )
    own_bias = lambda v, n: lax.dynamic_slice(v, (0, s * n), (1, n))
    own_up = own_bias(bias_up, ff)
    qkv_bias = jnp.concatenate(
        [
            own_bias(bias_qv[:, :width], inner),
            jnp.zeros((1, inner), f32),
            own_bias(bias_qv[:, width:], inner),
        ],
        axis=1,
    )
    x_pieces = spread(tokens)
    g_rows = jnp.stack(spread(after(grad_low, x_pieces[3])))
    h1, qkv = qkv_call(scal, x_pieces, wq, gain1, shift1, qkv_bias)
    o, lse = attend_call(scal, slopes, qkv, block)
    near, far = out_call(scal, o, w_o, out_first)
    got, across = reduce_rows(near, far)
    mid, h2 = mid_call(tokens, far, got, across, bias_out, gain2, shift2)
    h_pieces = spread(h2)
    y_near, y_far, d_near, d_far, a_all, du_all, h_all, g_all, up_sum = mlp_call(
        h_pieces, g_rows, w1, w_cols, own_up
    )
    got, across = reduce_rows(d_near, d_far)
    grad_down = outer_call(a_all, g_all, parts, "grad_fc2")
    grad_up = outer_call(h_all, du_all, 1, "grad_fc1")
    dmid, dbr, mid_sums = mid_back_call(mid, d_far, got, across, grad_low, gain2)

    b_pieces = spread(dbr)

    y_near = after(y_near, b_pieces[3])
    got, across = reduce_rows(y_near, y_far)
    output = (
        mid + ((y_far[1].astype(f32) + got[0].astype(f32)) + across.astype(f32) + bias_down)
    ).astype(bf16)

    do, grad_out = out_back_call(scal, b_pieces, o, w_o, out_first)
    dq, dk, dv = attend_back_call(scal, slopes, qkv, o, do, lse, block)
    near, far, merged, qkv_sums = qkv_back_call(scal, dq, dk, dv, wq)
    grad_qkv = outer_call(h1, merged, 1, "grad_qkv")

    def shared(part):
        if parts > 1:
            return lax.psum_scatter(part, "dp", scatter_dimension=0, tiled=False).astype(f32)
        return lax.psum_scatter(part, "dp", scatter_dimension=1, tiled=True).astype(f32)

    grad_down = shared(grad_down if parts > 1 else grad_down)
    grad_up = lax.psum_scatter(grad_up, "dp", scatter_dimension=0, tiled=True).astype(f32)
    got, across = reduce_rows(near, far)
    grad_tokens, in_sums = in_back_call(tokens, far, got, across, dmid, gain1)
    grad_out = shared(grad_out if parts > 1 else grad_out[0])
    grad_qkv = lax.psum_scatter(grad_qkv, "dp", scatter_dimension=0, tiled=True)
    grad_qkv = grad_qkv.astype(f32).reshape(w_qkv.shape)

    def own_slot(v, total):
        return lax.dynamic_update_slice(jnp.zeros((1, total), f32), v, (0, s * v.shape[1]))

    sums = (
        in_sums[0:1],
        in_sums[1:2],
        jnp.concatenate(
            [own_slot(qkv_sums[:, :inner], width), own_slot(qkv_sums[:, 2 * inner :], width)], axis=1
        ),
        mid_sums[2:3],
        mid_sums[0:1],
        mid_sums[1:2],
        own_slot(up_sum, seq_n * ff),
        mid_sums[3:4],
    )
    grads = jnp.concatenate([v.reshape(count, n) for v, n in zip(sums, sizes)], axis=1)
    grads = small_scatter(grads, count, seq_n).reshape(ends[-1])
    g_gain1, g_shift1, g_qv, g_bout, g_gain2, g_shift2, g_up, g_down = (
        grads[e - n : e] for e, n in zip(ends, sizes)
    )
    return (
        output,
        grad_tokens,
        g_gain1,
        g_shift1,
        grad_qkv,
        g_qv,
        grad_out,
        g_bout,
        g_gain2,
        g_shift2,
        grad_up,
        g_up,
        grad_down,
        g_down,
    )


def solution(mesh):
    rows = P(("dp", "seq"), None)
    vec = P(("dp", "seq"))
    merged = P("dp", None, "seq")
    return jax.shard_map(
        functools.partial(on_device, mesh.shape["dp"], mesh.shape["seq"]),
        mesh=mesh,
        in_specs=(
            rows, P("dp"), rows, vec, vec, merged, vec, P("seq", "dp"), vec, vec, vec,
            P("dp", "seq"), vec, P("seq", "dp"), vec,
        ),
        out_specs=(
            rows, rows, vec, vec, merged, vec, P("seq", "dp"), vec, vec, vec,
            P("dp", "seq"), vec, P("seq", "dp"), vec,
        ),
        check_vma=False,
    )
```

profile of v0, /device:TPU:0, one launch (start us, length us, event | category | flops | bytes accessed | tf_op | source)
XLA Modules:
  0.0 228.2 jit_solution(13600046744094628216)
XLA Ops:
  1.3 0.6 pad_add_fusion.scal
  1.9 0.6 dynamic_slice.3.slopes
  2.5 0.9 slice_bitcast_fusion.2
  3.4 0.7 pad_maximum_fusion.wq
  4.1 2.1 broadcast_select_fusion.g
  6.3 120.1 %fore.1 = (bf16[1536,1024]{1,0:T(8,128)(2,1)}, bf16[1536,768]{1,0:T(8,128)(2,1)}, bf16[1536,256]{1,0:T(8,128)(2,1)}, f32[2,8,1536]{2,1,0:T(8,128)}, bf16[8,128,7...) custom-call(s32[2]{0:T(128)} %pad_add_fusion.scal, ...), custom_call_target="tpu_custom_call" | custom-call | tf_op jit(solution)/shard_map/fore/pallas_call | solution.py:1437
  126.3 96.1 %back.1 = (bf16[384,1024]{1,0:T(8,128)(2,1)}, bf16[384,1024]{1,0:T(8,128)(2,1)}, f32[128,768]{1,0:T(8,128)}, f32[256,128]{1,0:T(8,128)}, f32[128,1024]{1,0:T(8,1...) custom-call(s32[2]{0:T(128)} %pad_add_fusion.scal, f32[4]{0:T(128)} %dynamic_slice.3.slopes, ...), custom_call_target="tpu_custom_call" | custom-call | tf_op jit(solution)/shard_map/back/pallas_call | solution.py:1789
  222.5 3.8 %finish.1 = (bf16[384,1024]{1,0:T(8,128)(2,1)}, bf16[384,1024]{1,0:T(8,128)(2,1)}, f32[128,3,256]{2,1,0:T(4,128)}, f32[256,128]{1,0:T(8,128)}, f32[128,1024]{1,0...) custom-call(s32[2]{0:T(128)} %pad_add_fusion.scal, ...), custom_call_target="tpu_custom_call" | custom-call | tf_op jit(solution)/shard_map/finish/pallas_call | solution.py:1867
  226.3 1.9 copy.29
  (2 shorter events, 0.0 us)
where the time goes:
time: 229 us; the launch traced here: 228 us
  Pallas kernels  220 us (96%)
  other arithmetic  3.46 us (2%)
  local copies, waits for them, and re-layouts  3.37 us (1%)
    pallas_call x1, Pallas kernels, fore_call(): pl.pallas_call(fore_body, out_shape=(shape((keys, width), bf16), shape((k...  120 us
    pallas_call x1, Pallas kernels, back_call(): pl.pallas_call(back_body, out_shape=(shape((rows, width), bf16), shape((r...  96.1 us

commit v1 on v0

--- a/solution.py
+++ b/solution.py
@@ -1019,7 +1019,7 @@
 
 
 def fore_body(
-    scal, slopes, wq, wo, x, v_up, v_qv, v_g1, v_s1, v_out, v_g2, v_s2, v_down, g, w1, w2,
+    lengths, slopes, wq, wo, x, v_up, v_qv, v_g1, v_s1, v_out, v_g2, v_s2, v_down, g, w1, w2,
     h1, qkv_out, o, lse, wq_all, flat, mid, gain1, bias_down, y_all, gw1, gw2, dmid, dbr, sums,
     up_sum,
     small, vectors, shift1, bias_qkv, bias_out, gain2, shift2, bias_up,
@@ -1039,14 +1039,16 @@
     halves = [slice(0, half_rows), slice(half_rows, rows)]
     column = lambda ref: lambda d: ref.at[:, pl.ds(pl.multiple_of(d * LANES, LANES), LANES)]
 
-    gather_q = Gather(wq, lambda d: wq_all.at[d], q_sem, dp, seq)
+    gather_q = Gather(wq, lambda d: wq_all.at[:, d], q_sem, dp, seq)
     gather_o = Gather(wo, column(flat), o_sem, dp, seq)
     gathers = [
         Gather(w1, lambda d: w1_all.at[d], w1_sem, dp, seq),
         Gather(w2, column(w2_flat), w2_sem, dp, seq),
     ]
     spread_x = Spread(x, rows_in, x_sem, dp, seq)
-    spread_g = Spread(g, g_rows, g_sem, dp, seq)
+    spread_g = Spread(g_rows.at[0], g_rows, g_sem, dp, seq)
+    length = lengths[0]
+    heads = 2 * pairs * seq
     at = 0
     for ref in (v_up, v_qv, v_g1, v_s1, v_out, v_g2, v_s2, v_down):
         small[:, at : at + ref.shape[1]] = ref[...].astype(f32)
@@ -1077,6 +1079,9 @@
     for i in range(1, 8):
         to_dp(i).start()
     gather_o.start()
+    keep_g.wait()
+    where = lax.broadcasted_iota(jnp.int32, (rows, width), 0) + seq * rows
+    g_rows[0] = jnp.where(where < length, g_rows[0], jnp.zeros((rows, width), bf16))
     spread_g.start()
     gather_q.hop(1)
     gather_q.hop(2)
@@ -1125,8 +1130,10 @@
         low = (unit * gain1[...] + shift1[...]).astype(bf16)
         h_stage[r % 2] = low
         h1_copy(r).start()
-        weight = wq_all[...].reshape(width, 3 * inner)
-        qkv[at, :] = (mm(low, weight) + bias_qkv[...]).astype(bf16)
+        for c in range(3):
+            cols = slice(c * inner, (c + 1) * inner)
+            value = mm(low, wq_all[c].reshape(width, inner)) + bias_qkv[:, cols]
+            qkv[at, cols] = value.astype(bf16)
         return carry
 
     lax.fori_loop(0, 4, project, 0)
@@ -1136,7 +1143,7 @@
         gather.hop(1)
     spread_g.forward()
     pos = lax.broadcasted_iota(jnp.int32, (keys, LANES), 0)
-    ramp[...] = jnp.where(pos < scal[1], pos.astype(f32), -1e33)
+    ramp[...] = jnp.where(pos < length, pos.astype(f32), -1e33)
     for p in range(pairs):
         vt[p] = qkv[:, 2 * inner + p * LANES : 2 * inner + (p + 1) * LANES].T
     gather_o.arrive()
@@ -1181,7 +1188,7 @@
                     k = qkv[0:length, k_lane]
                     outs, logs = [], []
                     for h in range(2):
-                        bias = ramp[0:length, :] * slopes[2 * p + h]
+                        bias = ramp[0:length, :] * slopes[heads + 2 * p + h]
                         s = scores(k, head_only(scaled, h), bias)
                         top = jnp.max(s, axis=0, keepdims=True)
                         e = jnp.exp(s - top)
@@ -1255,7 +1262,6 @@
     second_norm(0)
     up_sum[...] = jnp.zeros_like(up_sum)
     sums[...] = jnp.zeros_like(sums)
-    keep_g.wait()
     spread_g.near.wait_recv()
     spread_g.last.wait_recv()
     spread_g.drain()
@@ -1423,7 +1429,7 @@
         down_copy(width // chunk - 2 + k).wait()
 
 
-def fore_call(scal, slopes, wq, wo, x, small, g, w1, w2):
+def fore_call(lengths, slopes, wq, wo, x, small, g, w1, w2):
     rows, width = x.shape
     keys = 4 * rows
     inner, ff = wo.shape[0], w1.shape[1]
@@ -1441,7 +1447,7 @@
             shape((keys, 3 * inner), bf16),
             shape((keys, inner), bf16),
             shape((pairs, 8, keys), f32),
-            shape((8, *wq.shape), bf16),
+            shape((3, 8, *wq.shape[1:]), bf16),
             shape((inner, width), bf16),
             shape((rows, width), f32),
             shape((1, width), f32),
@@ -1489,26 +1495,38 @@
             vmem_limit_bytes=67043328, collective_id=4, has_side_effects=True
         ),
         name="fore",
-    )(scal, slopes, wq, wo, x, *(v.reshape(1, -1) for v in small), g, w1, w2)
+    )(lengths, slopes, wq, wo, x, *(v.reshape(1, -1) for v in small), g, w1, w2)
 
 
 def back_body(
-    scal, slopes, dbr, o, flat, qkv, lse, wq, h1, gw1, gw2, y_all, mid, bias_down, x, dmid,
-    gain1, mid_sums, up_sum,
-    output, grad, gq_out, go_out, gw1_out, gw2_out, small_out,
-    b_rows, y_far, do, go_sum, go_part, bias, kt, dk_sum, dv_sum, merged, qkv_sums, h_buf, turned,
+    lengths, slopes, dbr, o_in, flat_in, qkv_in, lse, wq_in, h1, gw1, gw2, y_all, mid_in, bias_down,
+    x_in, dmid_in, gain1, mid_sums, up_sum,
+    output, grad, gq_out, go_out, gw1_out, gw2_out, narrow_out, qv_out, up_out,
+    o, flat, qkv, wq, mid, x, dmid,
+    b_rows, y_far, do, go_sum, go_part, ramp, kt, dk_sum, dv_sum, merged, qkv_sums, h_buf, turned,
     gq_part, land_c, sum_y, land_y, y_land_c, y_sum, y_land_y,
     a_acc, a_x, a_land, a_sem, b_acc, b_x, b_land, b_sem, o_x, o_land, o_sem,
     q0_x, q0_land, q0_sem, q1_x, q1_land, q1_sem, q2_x, q2_land, q2_sem,
     small, small_land, own, seq_land,
-    b_row_sem, row_sems, y_sems, h_sem, small_sems, seq_sems, far_sem,
+    b_row_sem, row_sems, y_sems, h_sem, small_sems, seq_sems, far_sem, load_sem,
 ):
+    loads = [
+        pltpu.make_async_copy(src, dst, load_sem.at[i])
+        for i, (src, dst) in enumerate((
+            (dbr, b_rows.at[0]), (flat_in, flat), (o_in, o), (qkv_in, qkv), (mid_in, mid),
+            (wq_in, wq), (x_in, x), (dmid_in, dmid),
+        ))
+    ]
+    for copy in loads:
+        copy.start()
     dp, seq = lax.axis_index("dp"), lax.axis_index("seq")
     mate, across, far_mate = neighbours(seq)
     greet([((dp + i) % 8, seq) for i in range(1, 8)] + [(dp, p) for p in neighbours(seq)])
     rows, width = dbr.shape
     keys, inner = o.shape
+    length_all = lengths[0]
     pairs = inner // LANES
+    heads = 2 * pairs * seq
     scale = HEAD_DIM**-0.5
     chunk = 128
 
@@ -1548,22 +1566,6 @@
         copy.start()
     go_sum[...] = jnp.zeros_like(go_sum)
 
-    def out_back(r, carry):
-        if r >= 2:
-            spread_b.forward() if r == 2 else spread_b.last.wait_recv()
-        if r == 1:
-            spread_b.near.wait_recv()
-        at = pl.ds(pl.multiple_of(block_at(seq, r) * rows, rows), rows)
-        src = dbr if r == 0 else b_rows.at[r]
-        do[at, :] = mm_t(src[...], flat[...]).astype(bf16)
-        go_sum[...] += mm(o[at, :].T, src[...])
-        return carry
-
-    out_back(0, 0)
-    y_cores[1].start()
-    y_cores[0].start()
-    out_back(1, 0)
-
     def turn(i, carry):
         fetch_h(i).wait()
         turned[:, pl.ds(pl.multiple_of(i * rows, rows), rows)] = h_buf[i % 2].T
@@ -1574,7 +1576,6 @@
 
         return carry
 
-    lax.fori_loop(0, 4, turn, 0)
     small[...] = jnp.zeros_like(small)
     for d in range(8):
         at = slice(d * LANES, (d + 1) * LANES)
@@ -1583,81 +1584,106 @@
     for i in range(8):
         at = slice(i * LANES, (i + 1) * LANES)
         small[pl.ds(2 * seq + i // 4, 1), 7 + i % 4, :] = up_sum[:, at]
-    out_back(2, 0)
-    y_cores[1].wait_recv()
-    for copy in y_fetch:
+    dk_sum[...] = jnp.zeros_like(dk_sum)
+    dv_sum[...] = jnp.zeros_like(dv_sum)
+    pos = lax.broadcasted_iota(jnp.int32, (keys, LANES), 0)
+    ramp[...] = jnp.where(pos < length_all, pos.astype(f32), -1e33)
+    y_cores[1].start()
+    y_cores[0].start()
+    for copy in loads[:4]:
         copy.wait()
-    for i in range(rows // chunk):
-        at = slice(i * chunk, (i + 1) * chunk)
-        total = y_far[0, at, :].astype(f32) + y_land_c[1, at, :].astype(f32)
-        y_sum[at, :] = total.astype(bf16)
-    y_over.start()
-    out_back(3, 0)
+    for p in range(pairs):
+        kt[p] = qkv[:, inner + p * LANES : inner + (p + 1) * LANES].T
+
+    def attend_back(r, carry):
+        @pl.when(r == 1)
+        def _():
+            spread_b.near.wait_recv()
+
+        @pl.when(r == 2)
+        def _():
+            lax.fori_loop(0, 4, turn, 0)
+            spread_b.forward()
+            y_cores[1].wait_recv()
+            for copy in y_fetch:
+                copy.wait()
+            for i in range(rows // chunk):
+                at = slice(i * chunk, (i + 1) * chunk)
+                total = y_far[0, at, :].astype(f32) + y_land_c[1, at, :].astype(f32)
+                y_sum[at, :] = total.astype(bf16)
+            y_over.start()
+
+        @pl.when(r == 3)
+        def _():
+            spread_b.last.wait_recv()
+
+        c_now = block_at(seq, r)
+        at = pl.ds(pl.multiple_of(c_now * rows, rows), rows)
+        do[at, :] = mm_t(b_rows[r], flat[...]).astype(bf16)
+        go_sum[...] += mm(o[at, :].T, b_rows[r])
+        for c in range(keys // rows):
+
+            @pl.when(c_now == c)
+            def _(c=c):
+                length = (c + 1) * rows
+                at = slice(c * rows, length)
+
+                def one_pair(p, carry):
+                    lane = pl.ds(pl.multiple_of(p * LANES, LANES), LANES)
+                    k_lane = pl.ds(pl.multiple_of(inner + p * LANES, LANES), LANES)
+                    v_lane = pl.ds(pl.multiple_of(2 * inner + p * LANES, LANES), LANES)
+                    scaled = qkv[at, lane] * bf16(scale)
+                    g = do[at, lane]
+                    both = (g.astype(f32) * o[at, lane].astype(f32)).T
+                    k = qkv[0:length, k_lane]
+                    v = qkv[0:length, v_lane]
+                    outs = []
+                    for h in range(2):
+                        half = slice(h * HEAD_DIM, (h + 1) * HEAD_DIM)
+                        qm = head_only(scaled, h)
+                        gm = head_only(g, h)
+                        dot_row = jnp.sum(both[half], axis=0, keepdims=True)
+                        log = lse[p, h : h + 1, at]
+                        bias = ramp[0:length, :] * slopes[heads + 2 * p + h]
+                        e = jnp.exp(scores(k, qm, bias) - log)
+                        ds = (e * (mm_t(v, gm) - dot_row)).astype(bf16)
+                        dv_sum[p, 0:length, :] += mm(e.astype(bf16), gm)
+                        dk_sum[p, 0:length, :] += mm(ds, qm)
+                        outs.append(mm(kt[p, half, 0:length], ds))
+                    merged[at, lane] = (jnp.concatenate(outs, axis=0).T * scale).astype(bf16)
+                    return carry
+
+                lax.fori_loop(0, pairs, one_pair, 0)
+
+        @pl.when(r == 2)
+        def _():
+            sum_a.add_cross()
+            sum_a.stage(0)
+
+        return carry
+
+    lax.fori_loop(0, 4, attend_back, 0)
     for d in range(8):
         go_part[d] = go_sum[:, d * LANES : (d + 1) * LANES].astype(bf16)
     sum_o.start()
-    sum_a.add_cross()
-    sum_a.stage(0)
-
-    def one_pair(p, carry):
-        lane = pl.ds(pl.multiple_of(p * LANES, LANES), LANES)
-        k_lane = pl.ds(pl.multiple_of(inner + p * LANES, LANES), LANES)
-        v_lane = pl.ds(pl.multiple_of(2 * inner + p * LANES, LANES), LANES)
-        pos = lax.broadcasted_iota(jnp.int32, (keys, LANES), 0)
-        ramp = pos.astype(f32)
-        inside = pos < scal[1]
-        for h in range(2):
-            bias[h] = jnp.where(inside, ramp * slopes[2 * p + h], NEG)
-        kt[...] = qkv[:, k_lane].T
-        dk_sum[...] = jnp.zeros_like(dk_sum)
-        dv_sum[...] = jnp.zeros_like(dv_sum)
-        for c in range(keys // rows):
-            length = (c + 1) * rows
-            at = slice(c * rows, length)
-            scaled = qkv[at, lane] * bf16(scale)
-            g = do[at, lane]
-            both = (g.astype(f32) * o[at, lane].astype(f32)).T
-            k = qkv[0:length, k_lane]
-            v = qkv[0:length, v_lane]
-            outs = []
-            for h in range(2):
-                half = slice(h * HEAD_DIM, (h + 1) * HEAD_DIM)
-                qm = head_only(scaled, h)
-                gm = head_only(g, h)
-                dot_row = jnp.sum(both[half], axis=0, keepdims=True)
-                log = lse[p, h : h + 1, at]
-                e = jnp.exp(scores(k, qm, bias[h, 0:length, :]) - log)
-                ds = (e * (mm_t(v, gm) - dot_row)).astype(bf16)
-                dv_sum[0:length, :] += mm(e.astype(bf16), gm)
-                dk_sum[0:length, :] += mm(ds, qm)
-                outs.append(mm(kt[half, 0:length], ds))
-            merged[at, lane] = (jnp.concatenate(outs, axis=0).T * scale).astype(bf16)
-            if c == 2:
-
-                @pl.when(p == 1)
-                def _():
-                    sum_a.stage(2)
-
-        merged[:, k_lane] = dk_sum[...].astype(bf16)
-        merged[:, v_lane] = dv_sum[...].astype(bf16)
-
-        @pl.when(p == 0)
-        def _():
-            sum_a.stage(1)
-
-        return carry
-
-    lax.fori_loop(0, pairs, one_pair, 0)
+    for p in range(pairs):
+        lane = slice(p * LANES, (p + 1) * LANES)
+        merged[:, inner + p * LANES : inner + (p + 1) * LANES] = dk_sum[p].astype(bf16)
+        merged[:, 2 * inner + p * LANES : 2 * inner + (p + 1) * LANES] = dv_sum[p].astype(bf16)
     spread_b.drain()
-    sum_b.add_cross()
-    sum_b.stage(0)
+    sum_a.stage(1)
+    for copy in loads[4:]:
+        copy.wait()
     qkv_sums[...] = jnp.zeros_like(qkv_sums)
 
     def qkv_back(t, carry):
         rel = 3 - t
         at = pl.ds(pl.multiple_of(block_at(seq, rel) * rows, rows), rows)
         low = merged[at, :]
-        b_rows[rel] = mm_t(low, wq[...]).astype(bf16)
+        total = mm_t(low[:, :inner], wq[0].reshape(width, inner))
+        for c in range(1, 3):
+            total += mm_t(low[:, c * inner : (c + 1) * inner], wq[c].reshape(width, inner))
+        b_rows[rel] = total.astype(bf16)
         qkv_sums[...] += jnp.sum(low.astype(f32), axis=0, keepdims=True)
 
         @pl.when(t == 0)
@@ -1686,14 +1712,16 @@
         gq_part[j] = value.reshape(8, width // 8, inner)
         sums_q[j].start()
         if j == 0:
-            sum_o.add_cross()
-            sum_o.stage(0)
-            sum_b.stage(1)
+            sum_a.stage(2)
     for i in range(2):
         at = slice(i * LANES, (i + 1) * LANES)
         small[pl.ds(seq, 1), 2 + i, :] = qkv_sums[:, at]
         at = slice((4 + i) * LANES, (5 + i) * LANES)
         small[pl.ds(4 + seq, 1), 2 + i, :] = qkv_sums[:, at]
+    sum_b.add_cross()
+    sum_b.stage(0)
+    sum_o.add_cross()
+    sum_o.stage(0)
     sum_a.finish(gw2_out)
     y_cores[0].wait_recv()
     y_over.wait_recv()
@@ -1706,13 +1734,12 @@
         return carry
 
     lax.fori_loop(0, rows // chunk, out_step, 0)
+    sum_b.stage(1)
+    sum_o.stage(1)
     sums_q[0].add_cross()
     sums_q[0].stage(0)
-    sum_b.stage(2)
-    sum_o.stage(1)
     cores[0].wait_recv()
     over.wait_recv()
-    own[...] = jnp.zeros_like(own)
     qkv_gain = [jnp.zeros((1, width), f32), jnp.zeros((1, width), f32)]
     for i in range(rows // chunk):
         at = slice(i * chunk, (i + 1) * chunk)
@@ -1736,6 +1763,7 @@
 
     for i in range(1, 8):
         small_to(i).start()
+    sum_b.stage(2)
     sums_q[1].add_cross()
     sums_q[1].stage(0)
     sums_q[0].stage(1)
@@ -1763,9 +1791,22 @@
     sum_o.finish(go_out)
     for copy in group:
         copy.wait_recv()
-    small_out[...] = (own[...] + seq_land[0]) + (seq_land[1] + seq_land[2])
+    total = (own[...] + seq_land[0]) + (seq_land[1] + seq_land[2])
+    narrow = total[:, 0:32]
+    for i in range(1, 4):
+        narrow = jnp.where(seq == i, total[:, 32 * i : 32 * (i + 1)], narrow)
+    narrow_out[...] = narrow
+    value = total[2:3, 0:64]
+    for i in range(1, 4):
+        at = 64 * (i % 2)
+        value = jnp.where(seq == i, total[2 + i // 2 : 3 + i // 2, at : at + 64], value)
+    qv_out[...] = value
+    value = total[7:8]
+    for i in range(1, 4):
+        value = jnp.where(seq == i, total[7 + i : 8 + i], value)
+    up_out[...] = value
     for j in range(3):
-        sums_q[j].finish(gq_out.at[:, j * inner : (j + 1) * inner])
+        sums_q[j].finish(gq_out.at[j])
     for copy in group + cores + y_cores + [over, y_over]:
         copy.wait_send()
     for i in range(1, 8):
@@ -1775,40 +1816,49 @@
 
 
 def back_call(*args):
-    dbr, o, wo, qkv, lse, wq, h1, gw1, gw2 = args[2:11]
+    dbr, o, flat, qkv, lse, wq, h1, gw1, gw2 = args[2:11]
     rows, width = dbr.shape
     keys, inner = o.shape
+    pairs = inner // LANES
     sem = pltpu.SemaphoreType.DMA
     block = lambda dtype: pltpu.VMEM((rows, width), dtype)
     pair_rows = pltpu.VMEM((2, rows, width), bf16)
-    any_space = pl.BlockSpec(memory_space=pl.ANY)
-    specs = [SCALAR, SCALAR] + [WHOLE] * (len(args) - 2)
-    for at in (8, 9, 10, 11):
-        specs[at] = any_space
+    specs = [SCALAR, SCALAR] + [pl.BlockSpec(memory_space=pl.ANY)] * (len(args) - 2)
+    for at in (6, 13, 16, 17, 18):
+        specs[at] = WHOLE
     shape = jax.ShapeDtypeStruct
     return pl.pallas_call(
         back_body,
         out_shape=(
             shape((rows, width), bf16),
             shape((rows, width), bf16),
-            shape((width // 8, 3 * inner), f32),
+            shape((3, width // 8, inner), f32),
             shape((inner, LANES), f32),
             shape(gw1.shape[1:], f32),
             shape(gw2.shape[1:], f32),
-            shape((SMALL_ROWS, LANES), f32),
+            shape((SMALL_ROWS, 32), f32),
+            shape((1, 64), f32),
+            shape((1, LANES), f32),
         ),
         in_specs=specs,
-        out_specs=(WHOLE,) * 7,
+        out_specs=(WHOLE,) * 9,
         scratch_shapes=[
+            pltpu.VMEM(o.shape, bf16),
+            pltpu.VMEM(flat.shape, bf16),
+            pltpu.VMEM(qkv.shape, bf16),
+            pltpu.VMEM(wq.shape, bf16),
+            block(f32),
+            block(bf16),
+            block(f32),
             pltpu.VMEM((4, rows, width), bf16),
             pair_rows,
             pltpu.VMEM((keys, inner), bf16),
             pltpu.VMEM((inner, width), f32),
             pltpu.VMEM((8, inner, LANES), bf16),
-            pltpu.VMEM((2, keys, LANES), f32),
-            pltpu.VMEM((LANES, keys), bf16),
             pltpu.VMEM((keys, LANES), f32),
-            pltpu.VMEM((keys, LANES), f32),
+            pltpu.VMEM((pairs, LANES, keys), bf16),
+            pltpu.VMEM((pairs, keys, LANES), f32),
+            pltpu.VMEM((pairs, keys, LANES), f32),
             pltpu.VMEM((keys, 3 * inner), bf16),
             pltpu.VMEM((1, 3 * inner), f32),
             pair_rows,
@@ -1825,6 +1875,7 @@
             pltpu.VMEM((SMALL_ROWS, LANES), f32),
             pltpu.VMEM((3, SMALL_ROWS, LANES), f32),
             sem((2, 4)), sem((2, 3)), sem((2, 3)), sem((2,)), sem((2, 8)), sem((2, 3)), sem((2,)),
+            sem((8,)),
         ],
         compiler_params=pltpu.CompilerParams(
             vmem_limit_bytes=67043328, collective_id=3, has_side_effects=True
@@ -1834,49 +1885,40 @@
 
 
 def finish_body(
-    scal, output, grad, gq, go, gw1, gw2, small,
+    output, grad, gq, go, gw1, gw2, narrow, qv, up,
     output_out, grad_out, gq_out, go_out, gw1_out, gw2_out,
-    gain1, shift1, qv, bout, gain2, shift2, up, down,
+    gain1, shift1, qv_out, bout, gain2, shift2, up_out, down,
 ):
-    seq = scal[0]
-    output_out[...] = output[...]
-    grad_out[...] = grad[...]
-    go_out[...] = go[...]
-    gw1_out[...] = gw1[...]
-    gw2_out[...] = gw2[...]
-    cols = gq_out.shape[2]
-    for c in range(3):
-        gq_out[:, c, :] = gq[:, c * cols : (c + 1) * cols]
+    for src, dst in (
+        (output, output_out), (grad, grad_out), (gq, gq_out), (go, go_out), (gw1, gw1_out),
+        (gw2, gw2_out), (qv, qv_out), (up, up_out),
+    ):
+        dst[...] = src[...]
     for ref, row in ((gain1, 0), (shift1, 1), (bout, 4), (gain2, 5), (shift2, 6), (down, 11)):
-        n = ref.shape[1]
-        value = small[row : row + 1, 0:n]
-        for i in range(1, 4):
-            value = jnp.where(seq == i, small[row : row + 1, i * n : (i + 1) * n], value)
-        ref[...] = value
-    value = small[2:3, 0:64]
-    for i in range(1, 4):
-        at = 64 * (i % 2)
-        value = jnp.where(seq == i, small[2 + i // 2 : 3 + i // 2, at : at + 64], value)
-    qv[...] = value
-    up[...] = small[pl.ds(7 + seq, 1), :]
-
-
-def finish_call(scal, output, grad, gq, go, gw1, gw2, small):
-    one = lambda n: jax.ShapeDtypeStruct((1, n), f32)
+        ref[...] = narrow[row : row + 1, :]
+
+
+def finish_call(output, grad, gq, go, gw1, gw2, narrow, qv, up):
+    steps = 4
     like = lambda v: jax.ShapeDtypeStruct(v.shape, v.dtype)
+    cut = lambda v: pl.BlockSpec((v.shape[0] // steps, v.shape[1]), lambda i: (i, 0))
+    still = lambda v: pl.BlockSpec(v.shape, lambda i: (0, 0))
+    deep = pl.BlockSpec((3, gq.shape[1] // steps, gq.shape[2]), lambda i: (0, i, 0))
+    one = jax.ShapeDtypeStruct((1, 32), f32)
+    specs = [cut(output), cut(grad), deep, cut(go), cut(gw1), cut(gw2)]
     return pl.pallas_call(
         finish_body,
         out_shape=(
-            like(output), like(grad),
-            jax.ShapeDtypeStruct((gq.shape[0], 3, gq.shape[1] // 3), f32),
-            like(go), like(gw1), like(gw2),
-            one(32), one(32), one(64), one(32), one(32), one(32), one(LANES), one(32),
-        ),
-        in_specs=[SCALAR] + [WHOLE] * 7,
-        out_specs=(WHOLE,) * 14,
+            like(output), like(grad), like(gq), like(go), like(gw1), like(gw2),
+            one, one, like(qv), one, one, one, like(up), one,
+        ),
+        grid=(steps,),
+        in_specs=specs + [still(narrow), still(qv), still(up)],
+        out_specs=specs
+        + [still(one), still(one), still(qv), still(one), still(one), still(one), still(up), still(one)],
         compiler_params=params(),
         name="finish",
-    )(scal, output, grad, gq, go, gw1, gw2, small)
+    )(output, grad, gq, go, gw1, gw2, narrow, qv, up)
 
 
 def after(value, *others):
@@ -1912,6 +1954,7 @@
 
     scal = jnp.stack([s.astype(jnp.int32), length])
     slopes = 2.0 ** (-8.0 * (jnp.arange(heads, dtype=jnp.int32) + 1).astype(f32) / heads)
+    slopes_all = slopes
     slopes = lax.dynamic_slice(slopes, (s * (heads // seq_n),), (heads // seq_n,))
     valid = s * rows + jnp.arange(rows, dtype=jnp.int32) < length
     grad_low = jnp.where(valid[:, None], cotangent, jnp.zeros_like(cotangent))
@@ -1927,14 +1970,16 @@
         (
             h1, qkv, o, lse, wq, w_o, mid, gain1, bias_down, y_all, grad_up, grad_down, dmid, dbr,
             mid_sums, up_sum,
-        ) = fore_call(scal, slopes, wq_own, w_out, tokens, order, grad_low, w_fc1, w_fc2)
+        ) = fore_call(
+            lengths, slopes_all, jnp.transpose(w_qkv, (1, 0, 2)), w_out, tokens, order, cotangent,
+            w_fc1, w_fc2,
+        )
         results = back_call(
-            scal, slopes, dbr, o, w_o, qkv, lse, wq.reshape(width, 3 * inner), h1, grad_up,
-            grad_down, y_all, mid, bias_down, tokens, dmid, gain1, mid_sums, up_sum,
+            lengths, slopes_all, dbr, o, w_o, qkv, lse, wq, h1, grad_up, grad_down, y_all, mid,
+            bias_down, tokens, dmid, gain1, mid_sums, up_sum,
         )
-        output, grad_tokens, grad_qkv, grad_out, grad_up, grad_down, *vectors = finish_call(
-            scal, *results
-        )
+        output, grad_tokens, grad_qkv, grad_out, grad_up, grad_down, *vectors = finish_call(*results)
+        grad_qkv = jnp.transpose(grad_qkv, (1, 0, 2))
         g_gain1, g_shift1, g_qv, g_bout, g_gain2, g_shift2, g_up, g_down = (
             v.reshape(n) for v, n in zip(vectors, sizes)
         )

time: 229 us -> 221 us (0.965)
  local copies, waits for them, and re-layouts: 3.37 us -> 0 us
  other arithmetic: 3.46 us -> 0.52 us
where the time goes in v1:
time: 221 us
  Pallas kernels  219 us (99%)
    pallas_call x1, Pallas kernels, fore_call(): pl.pallas_call(fore_body, out_shape=(shape((keys, width), bf16), shape((k...  120 us
    pallas_call x1, Pallas kernels, back_call(): pl.pallas_call(back_body, out_shape=(shape((rows, width), bf16), shape((r...  94.3 us

profile of v1, /device:TPU:0, one launch (start us, length us, event | category | flops | bytes accessed | tf_op | source)
XLA Modules:
  0.0 220.7 jit_solution(9306905668858885923)
XLA Ops:
  1.3 0.5 multiply_power_fusion.slopes
  1.8 120.1 %fore.1 = (bf16[1536,1024]{1,0:T(8,128)(2,1)}, bf16[1536,768]{1,0:T(8,128)(2,1)}, bf16[1536,256]{1,0:T(8,128)(2,1)}, f32[2,8,1536]{2,1,0:T(8,128)}, bf16[3,8,128...) custom-call(s32[1]{0:T(128)S(6)} %copy.29.lengths, ...), custom_call_target="tpu_custom_call" | custom-call | tf_op jit(solution)/shard_map/fore/pallas_call | solution.py:1443
  121.9 94.3 %back.1 = (bf16[384,1024]{1,0:T(8,128)(2,1)}, bf16[384,1024]{1,0:T(8,128)(2,1)}, f32[3,128,256]{2,1,0:T(8,128)}, f32[256,128]{1,0:T(8,128)}, f32[128,1024]{1,0:T...) custom-call(s32[1]{0:T(128)S(6)} %copy.29.lengths, ...), custom_call_target="tpu_custom_call" | custom-call | tf_op jit(solution)/shard_map/back/pallas_call | solution.py:1830
  216.2 4.3 %finish.1 = (bf16[384,1024]{1,0:T(8,128)(2,1)}, bf16[384,1024]{1,0:T(8,128)(2,1)}, f32[3,128,256]{2,1,0:T(8,128)}, f32[256,128]{1,0:T(8,128)}, f32[128,1024]{1,0...) custom-call(bf16[384,1024]{1,0:T(8,128)(2,1)} %get-tuple-element.69., ...), custom_call_target="tpu_custom_call" | custom-call | tf_op jit(solution)/shard_map/finish/pallas_call | solution.py:1909

commit v2 on v1

--- a/solution.py
+++ b/solution.py
@@ -882,6 +882,127 @@
         ]
 
 
+class LineSum:
+    def __init__(self, part, acc, land, landx, sems, dp, seq):
+        self.part, self.acc, self.land, self.landx, self.sems = part, acc, land, landx, sems
+        self.seq, self.z, self.x = seq, dp // 2, dp % 2
+
+    def fetch(self, b):
+        return pltpu.make_async_copy(
+            self.part.at[pl.ds(2 * b, 2)], self.acc.at[b], self.sems.at[4, b]
+        )
+
+    def right(self, b, first):
+        slot = self.land.at[b + 1]
+        return remote(
+            self.part.at[pl.ds(2 * b, 2)] if first else slot,
+            slot,
+            self.sems.at[0, b],
+            self.sems.at[1, b],
+            2 * ((self.z + 1) % 4) + self.x,
+            self.seq,
+        )
+
+    def left(self, b, first):
+        slot = self.land.at[b]
+        return remote(
+            self.part.at[pl.ds(2 * b, 2)] if first else slot,
+            slot,
+            self.sems.at[2, b],
+            self.sems.at[3, b],
+            2 * ((self.z + 3) % 4) + self.x,
+            self.seq,
+        )
+
+    def start(self):
+        for i in range(3):
+
+            @pl.when(self.z == 0)
+            def _(i=i):
+                self.right(3 - i, True).start()
+
+            @pl.when(self.z == 3)
+            def _(i=i):
+                self.left(i, True).start()
+
+        for b in range(4):
+            self.fetch(b).start()
+
+    def ready(self):
+        for b in range(4):
+            self.fetch(b).wait()
+
+    def hop(self, k, b):
+        @pl.when(self.z == k)
+        def _():
+            self.right(b, False).wait_recv()
+            total = self.land[b + 1].astype(f32) + self.acc[b].astype(f32)
+            self.land[b + 1] = total.astype(bf16)
+            self.right(b, False).start()
+
+        c = 3 - b
+
+        @pl.when(self.z == 3 - k)
+        def _():
+            self.left(c, False).wait_recv()
+            total = self.land[c].astype(f32) + self.acc[c].astype(f32)
+            self.land[c] = total.astype(bf16)
+            self.left(c, False).start()
+
+    def cross(self):
+        z = self.z
+        return remote(
+            self.acc.at[z, 1 - self.x],
+            self.landx,
+            self.sems.at[5, 0],
+            self.sems.at[5, 1],
+            2 * z + (1 - self.x),
+            self.seq,
+        )
+
+    def merge(self):
+        z = self.z
+
+        @pl.when(z > 0)
+        def _():
+            self.right(z, False).wait_recv()
+            self.acc[z] = (self.acc[z].astype(f32) + self.land[z + 1].astype(f32)).astype(bf16)
+
+        @pl.when(z < 3)
+        def _():
+            self.left(z, False).wait_recv()
+            self.acc[z] = (self.acc[z].astype(f32) + self.land[z].astype(f32)).astype(bf16)
+
+        self.cross().start()
+
+    def finish(self, out):
+        self.cross().wait_recv()
+        out[...] = self.acc[self.z, self.x].astype(f32) + self.landx[...].astype(f32)
+
+    def drain(self):
+        self.cross().wait_send()
+        for k in range(3):
+
+            @pl.when(self.z == k)
+            def _(k=k):
+                for b in range(3, k, -1):
+                    self.right(b, k == 0).wait_send()
+
+            @pl.when(self.z == 3 - k)
+            def _(k=k):
+                for b in range(0, 3 - k):
+                    self.left(b, k == 0).wait_send()
+
+    @staticmethod
+    def scratch(m, n):
+        return [
+            pltpu.VMEM((4, 2, m, n), bf16),
+            pltpu.VMEM((5, 2, m, n), bf16),
+            pltpu.VMEM((m, n), bf16),
+            pltpu.SemaphoreType.DMA((6, 4)),
+        ]
+
+
 SMALL_ROWS = 16
 
 
@@ -977,6 +1098,98 @@
         return pltpu.SemaphoreType.DMA((6, 4))
 
 
+class CrossGather:
+    def __init__(self, own, slot, sems, dp, seq):
+        self.own, self.slot, self.sems = own, slot, sems
+        self.dp, self.seq, self.z, self.x = dp, seq, dp // 2, dp % 2
+
+    def along(self, k, step, side, src=None):
+        slot = self.slot(2 * k + (self.x + side) % 2)
+        return remote(
+            slot if src is None else src,
+            slot,
+            self.sems.at[side if step > 0 else 2 + side, k],
+            self.sems.at[4 + side, k],
+            2 * ((self.z + step + 4) % 4) + self.x,
+            self.seq,
+        )
+
+    def cross(self):
+        return remote(
+            self.own,
+            self.slot(self.dp),
+            self.sems.at[6, 0],
+            self.sems.at[6, 1],
+            2 * self.z + (1 - self.x),
+            self.seq,
+        )
+
+    def keep(self):
+        return pltpu.make_async_copy(self.own, self.slot(self.dp), self.sems.at[6, 2])
+
+    def both_ways(self, side, src=None):
+        z = self.z
+
+        @pl.when(z < 3)
+        def _():
+            self.along(z, 1, side, src).start()
+
+        @pl.when(z > 0)
+        def _():
+            self.along(z, -1, side, src).start()
+
+    def start(self):
+        self.cross().start()
+        self.both_ways(0, self.own)
+        self.keep().start()
+
+    def turn(self):
+        self.cross().wait_recv()
+        self.both_ways(1)
+
+    def hop(self, dist, side):
+        z = self.z
+
+        @pl.when(z - dist >= 0)
+        def _():
+            k = z - dist
+            self.along(k, 1, side).wait_recv()
+
+            @pl.when(z < 3)
+            def _():
+                self.along(k, 1, side).start()
+
+        @pl.when(z + dist <= 3)
+        def _():
+            k = z + dist
+            self.along(k, -1, side).wait_recv()
+
+            @pl.when(z > 0)
+            def _():
+                self.along(k, -1, side).start()
+
+    def arrive(self):
+        self.keep().wait()
+
+    def drain(self):
+        z = self.z
+        self.cross().wait_send()
+        for side in range(2):
+            for k in range(4):
+
+                @pl.when((z < 3) & (z >= k))
+                def _(k=k, side=side):
+                    self.along(k, 1, side).wait_send()
+
+                @pl.when((z > 0) & (z <= k))
+                def _(k=k, side=side):
+                    self.along(k, -1, side).wait_send()
+
+    @staticmethod
+    def scratch():
+        return pltpu.SemaphoreType.DMA((7, 4))
+
+
 class Spread:
     def __init__(self, own, rows, sems, dp, seq):
         mate, across = seq + 1 - 2 * (seq % 2), (seq + 2) % 4
@@ -1025,7 +1238,7 @@
     small, vectors, shift1, bias_qkv, bias_out, gain2, shift2, bias_up,
     rows_in, g_rows, h_stage, qkv, ramp, vt, part, land_c, sum_y, land_y, w1_all, w2_flat,
     a_all, du_all, turned, y_stage, up_stage, down_stage,
-    q_sem, o_sem, w1_sem, w2_sem, x_sem, g_sem, seq_sem, dp_sem, keep_sem, stage_sem, fwd, mlp, bwd,
+    q_sem, o_sem, w1_sem, w2_sem, low_sem, x_sem, g_sem, seq_sem, dp_sem, keep_sem, stage_sem, fwd, mlp, bwd,
 ):
     dp, seq = lax.axis_index("dp"), lax.axis_index("seq")
     mate, across, _ = neighbours(seq)
@@ -1037,14 +1250,18 @@
     ff = du_all.shape[1]
     half_rows = rows // 2
     halves = [slice(0, half_rows), slice(half_rows, rows)]
-    column = lambda ref: lambda d: ref.at[:, pl.ds(pl.multiple_of(d * LANES, LANES), LANES)]
+    lanes_of = lambda d: pl.ds(pl.multiple_of(d * LANES, LANES), LANES)
+    top, low = pl.ds(0, ff // 2), pl.ds(ff // 2, ff // 2)
 
     gather_q = Gather(wq, lambda d: wq_all.at[:, d], q_sem, dp, seq)
-    gather_o = Gather(wo, column(flat), o_sem, dp, seq)
+    gather_o = Gather(wo, lambda d: flat.at[:, lanes_of(d)], o_sem, dp, seq)
     gathers = [
         Gather(w1, lambda d: w1_all.at[d], w1_sem, dp, seq),
-        Gather(w2, column(w2_flat), w2_sem, dp, seq),
+        Gather(w2.at[top], lambda d: w2_flat.at[top, lanes_of(d)], w2_sem, dp, seq),
     ]
+    gather_low = CrossGather(
+        w2.at[low], lambda d: w2_flat.at[low, lanes_of(d)], low_sem, dp, seq
+    )
     spread_x = Spread(x, rows_in, x_sem, dp, seq)
     spread_g = Spread(g_rows.at[0], g_rows, g_sem, dp, seq)
     length = lengths[0]
@@ -1087,6 +1304,7 @@
     gather_q.hop(2)
     gather_o.hop(1)
     gather_q.hop(3)
+    gather_low.start()
     gather_o.hop(2)
     spread_x.forward()
     gather_o.hop(3)
@@ -1125,6 +1343,13 @@
         def _():
             h1_copy(r - 2).wait()
 
+        @pl.when(r == 2)
+        def _():
+            gather_low.turn()
+            for gather in gathers:
+                gather.hop(1)
+            gather_low.hop(1, 0)
+
         at = pl.ds(pl.multiple_of(block_at(seq, r) * rows, rows), rows)
         unit, _ = normalize(rows_in[r].astype(f32))
         low = (unit * gain1[...] + shift1[...]).astype(bf16)
@@ -1139,8 +1364,7 @@
     lax.fori_loop(0, 4, project, 0)
     qkv_copy = pltpu.make_async_copy(qkv, qkv_out, keep_sem.at[3])
     qkv_copy.start()
-    for gather in gathers:
-        gather.hop(1)
+    gather_low.hop(1, 1)
     spread_g.forward()
     pos = lax.broadcasted_iota(jnp.int32, (keys, LANES), 0)
     ramp[...] = jnp.where(pos < length, pos.astype(f32), -1e33)
@@ -1208,25 +1432,29 @@
         def _():
             for copy in rel_three:
                 copy.start()
+            for gather in gathers:
+                gather.hop(2)
+            gather_low.hop(2, 0)
 
         @pl.when(t == 1)
         def _():
             send_over(rel_three, over, 0)
             send_over(rel_three, over, 1)
-            for gather in gathers:
-                gather.hop(2)
+            gather_low.hop(2, 1)
 
         @pl.when(t == 2)
         def _():
             rel_one.start()
             for gather in gathers:
                 gather.hop(3)
+            gather_low.hop(3, 0)
 
         return carry
 
     lax.fori_loop(0, 4, attend, 0)
     gather_q.drain()
     gather_o.drain()
+    gather_low.hop(3, 1)
     rel_one.wait_recv()
 
     near, far, last = (
@@ -1265,7 +1493,7 @@
     spread_g.near.wait_recv()
     spread_g.last.wait_recv()
     spread_g.drain()
-    for gather in gathers:
+    for gather in gathers + [gather_low]:
         gather.arrive()
     for copy in [rel_one] + rel_three:
         copy.wait_send()
@@ -1419,7 +1647,7 @@
         copy.wait_send()
     for i in range(1, 8):
         to_dp(i).wait_send()
-    for gather in gathers:
+    for gather in gathers + [gather_low]:
         gather.drain()
     qkv_copy.wait()
     for k in range(2):
@@ -1488,6 +1716,7 @@
             pltpu.VMEM((2, 8, width // 8, 256), bf16),
             pltpu.VMEM((2, 2, ff, LANES), bf16),
             Gather.scratch(), Gather.scratch(), Gather.scratch(), Gather.scratch(),
+            CrossGather.scratch(),
             sem((2, 4)), sem((2, 4)), sem((2, 3)), sem((2, 8)), sem((4,)), sem((4, 2)),
             sem((2, 5)), sem((2, 6)), sem((2, 5)),
         ],
@@ -1505,7 +1734,7 @@
     o, flat, qkv, wq, mid, x, dmid,
     b_rows, y_far, do, go_sum, go_part, ramp, kt, dk_sum, dv_sum, merged, qkv_sums, h_buf, turned,
     gq_part, land_c, sum_y, land_y, y_land_c, y_sum, y_land_y,
-    a_acc, a_x, a_land, a_sem, b_acc, b_x, b_land, b_sem, o_x, o_land, o_sem,
+    a_acc, a_x, a_land, a_sem, b_acc, b_land, b_x, b_sem, o_x, o_land, o_sem,
     q0_x, q0_land, q0_sem, q1_x, q1_land, q1_sem, q2_x, q2_land, q2_sem,
     small, small_land, own, seq_land,
     b_row_sem, row_sems, y_sems, h_sem, small_sems, seq_sems, far_sem, load_sem,
@@ -1533,7 +1762,7 @@
     spread_b = Spread(dbr, b_rows, b_row_sem, dp, seq)
     spread_b.start()
     sum_a = GradSum(gw2, a_acc, a_x, a_land, a_sem, dp, seq)
-    sum_b = GradSum(gw1, b_acc, b_x, b_land, b_sem, dp, seq)
+    sum_b = LineSum(gw1, b_acc, b_land, b_x, b_sem, dp, seq)
     sum_o = GradSum(go_part, None, o_x, o_land, o_sem, dp, seq)
     sums_q = [
         GradSum(gq_part.at[0], None, q0_x, q0_land, q0_sem, dp, seq),
@@ -1655,8 +1884,15 @@
 
                 lax.fori_loop(0, pairs, one_pair, 0)
 
+        @pl.when(r == 1)
+        def _():
+            sum_b.ready()
+            sum_b.hop(1, 3)
+
         @pl.when(r == 2)
         def _():
+            sum_b.hop(1, 2)
+            sum_b.hop(2, 3)
             sum_a.add_cross()
             sum_a.stage(0)
 
@@ -1671,7 +1907,6 @@
         merged[:, inner + p * LANES : inner + (p + 1) * LANES] = dk_sum[p].astype(bf16)
         merged[:, 2 * inner + p * LANES : 2 * inner + (p + 1) * LANES] = dv_sum[p].astype(bf16)
     spread_b.drain()
-    sum_a.stage(1)
     for copy in loads[4:]:
         copy.wait()
     qkv_sums[...] = jnp.zeros_like(qkv_sums)
@@ -1706,23 +1941,22 @@
         return carry
 
     lax.fori_loop(0, 4, qkv_back, 0)
+    sum_b.merge()
     for j in range(3):
         cols = slice(j * inner, (j + 1) * inner)
         value = mm(turned[...], merged[:, cols]).astype(bf16)
         gq_part[j] = value.reshape(8, width // 8, inner)
         sums_q[j].start()
         if j == 0:
-            sum_a.stage(2)
+            sum_a.stage(1)
     for i in range(2):
         at = slice(i * LANES, (i + 1) * LANES)
         small[pl.ds(seq, 1), 2 + i, :] = qkv_sums[:, at]
         at = slice((4 + i) * LANES, (5 + i) * LANES)
         small[pl.ds(4 + seq, 1), 2 + i, :] = qkv_sums[:, at]
-    sum_b.add_cross()
-    sum_b.stage(0)
     sum_o.add_cross()
     sum_o.stage(0)
-    sum_a.finish(gw2_out)
+    sum_a.stage(2)
     y_cores[0].wait_recv()
     y_over.wait_recv()
 
@@ -1734,7 +1968,6 @@
         return carry
 
     lax.fori_loop(0, rows // chunk, out_step, 0)
-    sum_b.stage(1)
     sum_o.stage(1)
     sums_q[0].add_cross()
     sums_q[0].stage(0)
@@ -1763,7 +1996,6 @@
 
     for i in range(1, 8):
         small_to(i).start()
-    sum_b.stage(2)
     sums_q[1].add_cross()
     sums_q[1].stage(0)
     sums_q[0].stage(1)
@@ -1787,6 +2019,7 @@
     sums_q[2].stage(1)
     sums_q[1].stage(2)
     sums_q[2].stage(2)
+    sum_a.finish(gw2_out)
     sum_b.finish(gw1_out)
     sum_o.finish(go_out)
     for copy in group:
@@ -1867,7 +2100,7 @@
             pair_rows, block(bf16), block(bf16),
             pair_rows, block(bf16), block(bf16),
             *GradSum.scratch(*gw2.shape[1:], fetched=True),
-            *GradSum.scratch(*gw1.shape[1:], fetched=True),
+            *LineSum.scratch(*gw1.shape[1:]),
             *GradSum.scratch(inner, LANES),
             *(GradSum.scratch(width // 8, inner) * 3),
             pltpu.VMEM((8, SMALL_ROWS, LANES), f32),

time: 221 us -> 206 us (0.932)
  Pallas kernels: 219 us -> 204 us
    pallas_call x1, Pallas kernels: 94.3 us -> 81.8 us  [back_call(): pl.pallas_call(back_body, out_shape=(shape((rows, width), bf16), shape((r...]
    pallas_call x1, Pallas kernels: 120 us -> 118 us  [fore_call(): pl.pallas_call(fore_body, out_shape=(shape((keys, width), bf16), shape((k...]
where the time goes in v2:
time: 206 us
  Pallas kernels  204 us (99%)
    pallas_call x1, Pallas kernels, fore_call(): pl.pallas_call(fore_body, out_shape=(shape((keys, width), bf16), shape((k...  118 us
    pallas_call x1, Pallas kernels, back_call(): pl.pallas_call(back_body, out_shape=(shape((rows, width), bf16), shape((r...  81.8 us
    pallas_call x1, Pallas kernels, finish_call(): pl.pallas_call(finish_body, out_shape=(like(output), like(grad), like(gq)...  4.28 us

profile of v2, /device:TPU:0, one launch (start us, length us, event | category | flops | bytes accessed | tf_op | source)
XLA Modules:
  0.0 205.7 jit_solution(12032278975912751392)
XLA Ops:
  1.3 0.5 multiply_power_fusion.slopes
  1.8 117.5 %fore.1 = (bf16[1536,1024]{1,0:T(8,128)(2,1)}, bf16[1536,768]{1,0:T(8,128)(2,1)}, bf16[1536,256]{1,0:T(8,128)(2,1)}, f32[2,8,1536]{2,1,0:T(8,128)}, bf16[3,8,128...) custom-call(s32[1]{0:T(128)S(6)} %copy.29.lengths, ...), custom_call_target="tpu_custom_call" | custom-call | tf_op jit(solution)/shard_map/fore/pallas_call | solution.py:1671
  119.4 81.8 %back.1 = (bf16[384,1024]{1,0:T(8,128)(2,1)}, bf16[384,1024]{1,0:T(8,128)(2,1)}, f32[3,128,256]{2,1,0:T(8,128)}, f32[256,128]{1,0:T(8,128)}, f32[128,1024]{1,0:T...) custom-call(s32[1]{0:T(128)S(6)} %copy.29.lengths, ...), custom_call_target="tpu_custom_call" | custom-call | tf_op jit(solution)/shard_map/back/pallas_call | solution.py:2063
  201.2 4.3 %finish.1 = (bf16[384,1024]{1,0:T(8,128)(2,1)}, bf16[384,1024]{1,0:T(8,128)(2,1)}, f32[3,128,256]{2,1,0:T(8,128)}, f32[256,128]{1,0:T(8,128)}, f32[128,1024]{1,0...) custom-call(bf16[384,1024]{1,0:T(8,128)(2,1)} %get-tuple-element.69., ...), custom_call_target="tpu_custom_call" | custom-call | tf_op jit(solution)/shard_map/finish/pallas_call | solution.py:2142
